TPU v7x, 32 devices: a whole 2x2x4 slice. The times are simulated.
32 devices in a mesh: cone: 4 (over y, x), con: 8 (over z, core).
Axes of the slice: x: 2, y: 2, z: 4, core: 2. Of those that a mesh axis runs over, the one named last changes fastest.
Arguments:
- vectors: bfloat16 [4, 8192, 1024], P('cone', 'con'), may hold values from -0.1875 to 0.1875
- primal: bfloat16 [4, 1024, 1024], P('cone'), may hold values from -8 to 8, as said below
- dual_inverse: bfloat16 [4, 1024, 1024], P('cone'), may hold values from -8 to 8, as said below
- touches: int32 [4, 8], P('cone'), may hold values from 0 to 1, as said below
Outputs:
- slab: float32 [2048, 8192], P('cone', 'con')
Inputs may be any that keep to these rules, and one draw needn't show every extreme that they name: `primal`: symmetric and positive definite in every cone. `dual_inverse`: symmetric and positive definite in every cone. Every constraint block touches at least one cone.
All inputs are finite; a program needn't handle non-finite values.
Results may differ from a plain program's by a relative error of at most 0.00079.
Values may be sent and summed in bfloat16 or wider, within the bound.
No kernel may reach another device: no remote copies, remote signals or barrier semaphores. Data moves between devices by JAX's collectives and lax.ppermute only.
A program may use at most 128 MiB of HBM per device.

v0:
```python
import functools
import math

import jax
import jax.numpy as jnp
from jax import lax
from jax.experimental import pallas as pl
from jax.experimental.pallas import tpu as pltpu
from jax.sharding import PartitionSpec as P


PANEL = 512
TILE = 128
SUB = 8
STEPS = 128
LEVELS = 32767.0
OCTAVE = math.log(2.0) / STEPS
HI = lax.Precision.HIGHEST
ROWS_T = (((1,), (1,)), ((), ()))
COLS_T = (((0,), (0,)), ((), ()))
PLAIN = (((1,), (0,)), ((), ()))
F32 = jnp.float32
BF16 = jnp.bfloat16
I16 = jnp.int16


def in_vmem(count):
    return [pl.BlockSpec(memory_space=pltpu.VMEM)] * count


def in_smem():
    return pl.BlockSpec(memory_space=pltpu.SMEM)


def shaped(rows, columns, dtype):
    return jax.ShapeDtypeStruct((rows, columns), dtype)


def encode(value, out_ref, start):
    rows = value.shape[0]
    top = jnp.max(jnp.abs(value), axis=0, keepdims=True)
    level = jnp.ceil(jnp.log(jnp.maximum(top, 1e-37)) * (1.0 / OCTAVE))
    scaled = value * jnp.exp(level * -OCTAVE) * LEVELS
    whole = jnp.round(jnp.clip(scaled, -LEVELS, LEVELS)).astype(jnp.int32)
    out_ref[start : start + rows, :] = whole.astype(I16)
    levels = jnp.broadcast_to(level, (SUB, value.shape[1])).astype(jnp.int32)
    out_ref[start + rows : start + rows + SUB, :] = levels.astype(I16)


def decode(ref, start, rows):
    whole = ref[start : start + rows, :].astype(jnp.int32).astype(F32)
    level = ref[start + rows : start + rows + SUB, :].astype(jnp.int32).astype(F32)[0:1]
    return whole * (jnp.exp(level * OCTAVE) * (1.0 / LEVELS))


def factor_tile(a):
    groups = TILE // SUB
    rows = lax.broadcasted_iota(jnp.int32, (SUB, TILE), 0)
    lanes = lax.broadcasted_iota(jnp.int32, (SUB, TILE), 1)
    left = [a[g * SUB : (g + 1) * SUB, :] for g in range(groups)]
    right = [jnp.where(lanes == rows + g * SUB, 1.0, 0.0).astype(F32) for g in range(groups)]
    spread = lambda x, j: jnp.broadcast_to(x[:, j : j + 1], (SUB, TILE))
    flat = lambda x, i: jnp.broadcast_to(x[i : i + 1, :], (SUB, TILE))
    first = [spread(x, 0) for x in left]
    second = [spread(x, 1) for x in left]
    scales = [None] * groups
    for j in range(0, TILE, 2):
        g0, i0 = divmod(j, SUB)
        corner, side, end = flat(first[g0], i0), flat(first[g0], i0 + 1), flat(second[g0], i0 + 1)
        by_first = 1.0 / corner
        by_second = corner * (1.0 / (corner * end - side * side))
        slope = side * by_first
        scale = jnp.where(rows == i0, by_first, by_second)
        scales[g0] = scale if i0 == 0 else jnp.where(rows >= i0, scale, scales[g0])
        left_0, right_0 = flat(left[g0], i0), flat(right[g0], i0)
        left_1 = flat(left[g0], i0 + 1) - slope * left_0
        right_1 = flat(right[g0], i0 + 1) - slope * right_0
        more = j + 2 < TILE
        if more:
            g1, i1 = divmod(j + 2, SUB)
            ahead_0 = [spread(left[g], j + 2) if g >= g1 else None for g in range(groups)]
            ahead_1 = [spread(left[g], j + 3) if g >= g1 else None for g in range(groups)]
            p0, q0 = flat(first[g1], i1), flat(first[g1], i1 + 1)
            p1 = flat(second[g1], i1) - slope * p0
            q1 = flat(second[g1], i1 + 1) - slope * q0
        following = [None] * groups, [None] * groups
        for g in range(g0, groups):
            ratio_0 = first[g] * by_first
            ratio_1 = (second[g] - first[g] * slope) * by_second
            if g == g0:
                ratio_0 = jnp.where(rows > i0, ratio_0, 0.0)
                ratio_1 = jnp.where(rows > i0 + 1, ratio_1, 0.0)
            if more and g >= g1:
                following[0][g] = (ahead_0[g] - ratio_0 * p0) - ratio_1 * p1
                following[1][g] = (ahead_1[g] - ratio_0 * q0) - ratio_1 * q1
            left[g] = (left[g] - ratio_0 * left_0) - ratio_1 * left_1
            right[g] = (right[g] - ratio_0 * right_0) - ratio_1 * right_1
        first, second = following
    return jnp.concatenate([r * jnp.sqrt(p) for r, p in zip(right, scales)], axis=0)


def eliminate_kernel(first, last, work_in, x_in, work, x_ref):
    del work_in, x_in
    tiles = work.shape[0] // TILE

    def step(p, carry):
        here = pl.ds(pl.multiple_of(p * TILE, TILE), TILE)
        tile = factor_tile(work[here, here])
        upper = jnp.dot(tile, work[here, :], precision=HI, preferred_element_type=F32)
        solved = jnp.dot(tile, x_ref[here, :], precision=HI, preferred_element_type=F32)
        x_ref[here, :] = solved
        for q in range(first + 1, tiles):

            @pl.when(q > p)
            def _():
                below = slice(q * TILE, (q + 1) * TILE)
                part = upper[:, below]
                work[below, :] -= lax.dot_general(
                    part, upper, COLS_T, precision=HI, preferred_element_type=F32
                )
                x_ref[below, :] -= lax.dot_general(
                    part, solved, COLS_T, precision=HI, preferred_element_type=F32
                )

        return carry

    lax.fori_loop(first, last, step, 0)


def eliminate(work, x, first, last):
    size = work.shape[0]
    return pl.pallas_call(
        functools.partial(eliminate_kernel, first, last),
        out_shape=(shaped(size, size, F32),) * 2,
        in_specs=in_vmem(2),
        out_specs=tuple(in_vmem(2)),
        input_output_aliases={0: 0, 1: 1},
        compiler_params=pltpu.CompilerParams(vmem_limit_bytes=6 << 20),
    )(work, x)


def square_kernel(*refs):
    *half_refs, work, x_ref, square = refs
    size = x_ref.shape[0]
    owners = len(half_refs)
    width = size // owners
    core = lax.rem(lax.axis_index("con"), owners)
    for s, half_ref in enumerate(half_refs):
        where = lax.rem(core + s, owners) * width
        at = pl.ds(pl.multiple_of(where, TILE), width)
        for g in range(size // TILE):
            square[g * TILE : (g + 1) * TILE, at] = decode(half_ref, g * (TILE + SUB), TILE)
    rows = lax.broadcasted_iota(jnp.int32, (size, size), 0)
    columns = lax.broadcasted_iota(jnp.int32, (size, size), 1)
    value = square[...]
    value = (value + value.T) * 0.5
    diagonal = jnp.where(rows == columns, value, 0.0)
    across = lax.rsqrt(jnp.sum(diagonal, axis=0, keepdims=True))
    down = lax.rsqrt(jnp.sum(diagonal, axis=1, keepdims=True))
    work[...] = value * across * down
    x_ref[...] = jnp.where(rows == columns, across, 0.0)


def weigh(rows_ref, primal_ref, dual_ref, by_primal, by_dual):
    def part(i, carry):
        half = primal_ref.shape[1] // 2
        at = pl.ds(pl.multiple_of(i * half, half), half)
        for source, target in ((primal_ref, by_primal), (dual_ref, by_dual)):
            value = jnp.dot(rows_ref[...], source[:, at], preferred_element_type=F32)
            target[:, at] = value.astype(BF16)
        return carry

    lax.fori_loop(0, 2, part, 0)


def hadamard(by_primal, by_dual, columns):
    return lax.dot_general(
        by_primal, columns, ROWS_T, preferred_element_type=F32
    ) * lax.dot_general(by_dual, columns, ROWS_T, preferred_element_type=F32)


def split(value):
    high = value.astype(BF16)
    return high, (value - high.astype(F32)).astype(BF16)


def product(left, right, contract):
    dot = functools.partial(
        lax.dot_general, dimension_numbers=contract, preferred_element_type=F32
    )
    left_high, left_low = left
    right_high, right_low = right
    return dot(left_high, right_high) + (dot(left_high, right_low) + dot(left_low, right_high))


def mask_kernel(touches_ref, rows_ref, out_ref, flags, arrived):
    count = out_ref.shape[0]
    copies = [
        pltpu.make_async_copy(touches_ref, flags, arrived.at[0]),
        pltpu.make_async_copy(rows_ref.at[pl.ds(0, count), :], out_ref, arrived.at[1]),
    ]
    for copy in copies:
        copy.start()
    for copy in copies:
        copy.wait()
    out_ref[...] = out_ref[...] * flags[0, lax.axis_index("con")].astype(BF16)


def pick_kernel(owners, chips, *refs):
    *in_refs, out_ref = refs
    chip = lax.div(lax.axis_index("con"), owners)
    for in_ref, members in zip(in_refs, chips):
        for member in members:

            @pl.when(chip == member)
            def _():
                out_ref[...] = in_ref[...]


def assemble(part_refs, rows):
    owners = len(part_refs)
    count = part_refs[0].shape[0]
    core = lax.rem(lax.axis_index("con"), owners)
    for s, part_ref in enumerate(part_refs):
        where = pl.multiple_of(lax.rem(core + s, owners) * count, count)
        rows[pl.ds(where, count), :] = part_ref[...]


def panel_step(chip):
    return jnp.minimum(chip, 2)


def terms_kernel(owners, cones, touches_ref, *refs):
    part_refs = refs[:owners]
    primal_ref, dual_ref, columns_ref, own_ref = refs[owners : owners + 4]
    code_refs = refs[owners + 4 : owners + 3 + cones]
    lead_refs = refs[owners + 3 + cones : -4]
    rows, value_ref, p_ref, d_ref = refs[-4:]
    assemble(part_refs, rows)
    weigh(rows, primal_ref, dual_ref, p_ref, d_ref)
    flag = touches_ref[0, lax.axis_index("con")].astype(F32)
    value_ref[...] = hadamard(p_ref[...], d_ref[...], columns_ref[...]) * flag
    share = own_ref.shape[0]
    cone = lax.axis_index("cone")
    own_ref[...] = value_ref[pl.ds(pl.multiple_of(cone * share, share), share), :]
    for u, code_ref in enumerate(code_refs, 1):
        other = jnp.bitwise_xor(cone, u) * share
        encode(value_ref[pl.ds(pl.multiple_of(other, share), share), :], code_ref, 0)
    if lead_refs:
        lead_ref, lead_code_ref = lead_refs
        value = value_ref[:, : lead_ref.shape[1]]
        lead_ref[...] = value
        encode_square(value, lead_code_ref)


def encode_square(value, code_ref):
    for g in range(value.shape[0] // TILE):
        encode(value[g * TILE : (g + 1) * TILE], code_ref, g * (TILE + SUB))


def sum_half_kernel(own_ref, *refs):
    *code_refs, out_ref = refs
    for g in range(own_ref.shape[0] // TILE):
        total = own_ref[g * TILE : (g + 1) * TILE, :]
        for code_ref in code_refs:
            total = total + decode(code_ref, g * (TILE + SUB), TILE)
        encode(total, out_ref, g * (TILE + SUB))


def total_of(parts):
    own_ref, *code_refs = parts
    total = own_ref[...]
    for code_ref in code_refs:
        total = total + decode(code_ref, 0, total.shape[0])
    return total


def sum_panel_kernel(owners, cones, steps, *refs):
    sum_ref, out_ref = refs[-2:]
    step = panel_step(lax.div(lax.axis_index("con"), owners))
    for s in range(steps):

        @pl.when(step == s)
        def _():
            total = total_of(refs[s * cones : (s + 1) * cones])
            sum_ref[...] = total
            encode(total, out_ref, 0)


def sum_rest_kernel(owners, cones, order_ref, *refs):
    cone = lax.axis_index("cone")
    chip = lax.div(lax.axis_index("con"), owners)
    inputs = refs[: cones * cones]
    own_ref, *code_refs = refs[cones * cones : cones * cones + cones]
    sums = refs[-1]
    for s in range(cones):
        block = order_ref[chip, s]

        @pl.when(block != 0)
        def _():
            sums[block] = total_of(inputs[s * cones : (s + 1) * cones])

    @pl.when(cone != 0)
    def _():
        own_ref[...] = sums[cone]

    for u, code_ref in enumerate(code_refs, 1):
        other = jnp.bitwise_xor(cone, u)

        @pl.when(other != 0)
        def _():
            encode(sums[other], code_ref, 0)


def gather_panel_kernel(own_ref, *refs):
    *code_refs, panel_ref, lead_ref = refs
    share = own_ref.shape[0]
    cone = lax.axis_index("cone")
    panel_ref[pl.ds(pl.multiple_of(cone * share, share), share), :] = own_ref[...]
    for u, code_ref in enumerate(code_refs, 1):
        other = jnp.bitwise_xor(cone, u) * share
        panel_ref[pl.ds(pl.multiple_of(other, share), share), :] = decode(code_ref, 0, share)
    width = lead_ref.shape[1]
    encode_square(panel_ref[:, :width], lead_ref)


def pick_lead_kernel(owners, *refs):
    *in_refs, out_ref = refs
    chip = lax.div(lax.axis_index("con"), owners)
    step = jnp.bitwise_xor(chip, lax.axis_index("cone"))
    for d, in_ref in enumerate(in_refs):

        @pl.when(step == d)
        def _():
            out_ref[...] = in_ref[...]


def rows_kernel(inverse_ref, panel_ref, *refs):
    *lead_refs, factor_ref, row_ref, lead = refs
    owners = len(lead_refs)
    width = lead_refs[0].shape[1]
    core = lax.rem(lax.axis_index("con"), owners)
    for s, lead_ref in enumerate(lead_refs):
        where = pl.ds(pl.multiple_of(lax.rem(core + s, owners) * width, width), width)
        for g in range(panel_ref.shape[0] // TILE):
            lead[g * TILE : (g + 1) * TILE, where] = decode(lead_ref, g * (TILE + SUB), TILE)
    inverse = split(inverse_ref[...])
    factor_ref[...] = product(inverse, split(panel_ref[...]), PLAIN)
    row_ref[...] = product(inverse, split(lead[...]), PLAIN)


def update_kernel(owners, width, factor_ref, row_ref, own_ref, *refs):
    *code_refs, out_ref = refs
    share = own_ref.shape[0]
    cone = lax.axis_index("cone")
    pivots = lax.axis_index("con") < owners

    @pl.when(cone == 0)
    def _():
        out_ref[...] = factor_ref[...]

    @pl.when(cone != 0)
    def _():
        out_ref[pl.ds(pl.multiple_of(cone * share, share), share), :] = own_ref[...]
        for u, code_ref in enumerate(code_refs, 1):
            other = jnp.bitwise_xor(cone, u) * share
            out_ref[pl.ds(pl.multiple_of(other, share), share), :] = decode(code_ref, 0, share)
        change = product(split(row_ref[...]), split(factor_ref[...]), COLS_T)
        columns = lax.broadcasted_iota(jnp.int32, out_ref.shape, 1)
        out_ref[...] = jnp.where((columns < width) & pivots, 0.0, out_ref[...] - change)


def call(kernel, out_shape, operands, scratch=(), limit=16, scalars=0):
    return pl.pallas_call(
        kernel,
        out_shape=out_shape,
        in_specs=[in_smem()] * scalars + in_vmem(len(operands) - scalars),
        out_specs=jax.tree.map(lambda _: pl.BlockSpec(memory_space=pltpu.VMEM), out_shape),
        scratch_shapes=scratch,
        compiler_params=pltpu.CompilerParams(vmem_limit_bytes=limit << 20),
    )(*operands)


def gather_plan(chips):
    near = ("near", "own", [(z, z ^ 1) for z in range(chips)])
    if chips == 4:
        return [
            near,
            ("middle", "own", [(1, 2), (2, 1)]),
            ("far", "own", [(0, 3), (3, 0)]),
            ("pass_near", "near", [(1, 2), (2, 1)]),
            ("pass_middle", "middle", [(1, 0), (2, 3)]),
        ]
    plan = [near]
    for phase in range(chips // 2):
        for d in reversed(range(2, chips)):
            sources = sorted({phase, chips - 1 - phase})
            plan.append((f"phase_{phase}_{d}", "own", [(b, b ^ d) for b in sources]))
    return plan


def arrivals(chips):
    held = {"own": {z: z for z in range(chips)}}
    for name, sent, moves in gather_plan(chips):
        held[name] = {target: held[sent][source] for source, target in moves}
    return [
        {held[name][z]: name for name, _, _ in gather_plan(chips) if z in held[name]}
        for z in range(chips)
    ]


def block_order(chip, chips):
    names = [name for name, _, _ in gather_plan(chips)]
    by = arrivals(chips)[chip]
    rest = [b for b in range(chips) if b not in (chip, chip ^ 1)]
    return [chip, chip ^ 1] + sorted(rest, key=lambda b: (b != 0, names.index(by[b])))


def shards(vectors, primal, dual_inverse, touches):
    con_count = lax.axis_size("con")
    cones = lax.axis_size("cone")
    per_block, order_n = vectors.shape[1:]
    row_dev = PANEL * cones // con_count
    owners = con_count // cones
    share = PANEL // cones
    steps = min(cones, 3)
    columns, primal_block, dual_block = vectors[0], primal[0], dual_inverse[0]
    order = [block_order(z, cones) for z in range(cones)]

    def exchange(codes, pairs=lambda u: [(i, i ^ u) for i in range(cones)]):
        return [lax.ppermute(code, "cone", pairs(u)) for u, code in enumerate(codes, 1)]

    def along(value, moves):
        pairs = [(a * owners + i, b * owners + i) for a, b in moves for i in range(owners)]
        return lax.ppermute(value, "con", pairs)

    def beside(value):
        swaps = [value]
        for s in range(1, owners):
            pairs = [
                (g * owners + i, g * owners + (i - s) % owners)
                for g in range(cones)
                for i in range(owners)
            ]
            swaps.append(lax.ppermute(value, "con", pairs))
        return swaps

    in_hbm = pl.BlockSpec(memory_space=pltpu.MemorySpace.HBM)
    own_rows = pl.pallas_call(
        mask_kernel,
        out_shape=shaped(row_dev, order_n, BF16),
        in_specs=[in_hbm, in_hbm],
        out_specs=pl.BlockSpec(memory_space=pltpu.VMEM),
        scratch_shapes=[
            pltpu.SMEM(touches.shape, jnp.int32),
            pltpu.SemaphoreType.DMA((2,)),
        ],
        compiler_params=pltpu.CompilerParams(vmem_limit_bytes=2 << 20),
        cost_estimate=pl.CostEstimate(flops=10**10, transcendentals=0, bytes_accessed=10**6),
        name="mask_rows",
    )(touches, pltpu.with_memory_space_constraint(columns, pltpu.MemorySpace.HBM))
    parts = [beside(own_rows)]
    arrived = {"own": own_rows}
    for name, sent, moves in gather_plan(cones):
        arrived[name] = along(arrived[sent], moves)

    for step in range(1, cones):
        wanted = {}
        for z in range(cones):
            wanted.setdefault(arrivals(cones)[z][order[z][step]], []).append(z)
        keys = sorted(wanted)
        mine = call(
            functools.partial(pick_kernel, owners, [wanted[key] for key in keys]),
            shaped(row_dev, order_n, BF16),
            tuple(arrived[key] for key in keys),
            limit=4,
        )
        parts.append(beside(mine))

    coded_square = (PANEL // TILE) * (TILE + SUB)
    terms_shape = (shaped(share, per_block, F32),) + (shaped(share + SUB, per_block, I16),) * (
        cones - 1
    )
    lead_shape = (shaped(PANEL, row_dev, F32), shaped(coded_square, row_dev, I16))
    summed = []
    for step in range(cones):
        first, *codes = call(
            functools.partial(terms_kernel, owners, cones),
            terms_shape + (lead_shape if step == 0 else ()),
            (touches, *parts[step], primal_block, dual_block, columns),
            [
                pltpu.VMEM((PANEL, order_n), BF16),
                pltpu.VMEM((PANEL, per_block), F32),
                pltpu.VMEM((PANEL, order_n), BF16),
                pltpu.VMEM((PANEL, order_n), BF16),
            ],
            18,
            1,
        )
        if step == 0:
            half_own, half_code = codes[cones - 1 :]
        summed.append([first] + exchange(codes[: cones - 1]))

    grid = ("cone", "con")
    half_codes = [
        lax.ppermute(
            half_code,
            grid,
            [(c * con_count + i, (c ^ u) * con_count + i) for c in range(cones) for i in range(owners)],
        )
        for u in range(1, cones)
    ]
    half = call(
        sum_half_kernel, shaped(coded_square, row_dev, I16), (half_own, *half_codes), limit=4
    )
    halves = [half] + [along(half, [(0, d)]) for d in range(1, cones)]
    half = call(
        functools.partial(pick_kernel, owners, [[d] for d in range(cones)]),
        shaped(coded_square, row_dev, I16),
        tuple(halves),
        limit=4,
    )
    work, inverse = call(
        square_kernel,
        (shaped(PANEL, PANEL, F32),) * 2,
        tuple(beside(half)),
        [pltpu.VMEM((PANEL, PANEL), F32)],
        6,
    )
    tiles = PANEL // TILE
    work, inverse = eliminate(work, inverse, 0, tiles // 2)
    work, inverse = eliminate(work, inverse, tiles // 2, tiles)

    panel_own, panel_code = call(
        functools.partial(sum_panel_kernel, owners, cones, steps),
        (shaped(share, per_block, F32), shaped(share + SUB, per_block, I16)),
        tuple(part for group in summed[:steps] for part in group),
        limit=8,
    )
    panel, lead = call(
        gather_panel_kernel,
        (shaped(PANEL, per_block, F32), shaped(coded_square, row_dev, I16)),
        (panel_own, *exchange([panel_code] * (cones - 1))),
        limit=6,
    )
    leads = [lead]
    for d in range(1, cones):
        pairs = [
            (c * con_count + c * owners + i, c * con_count + (c ^ d) * owners + i)
            for c in range(1, cones)
            for i in range(owners)
        ]
        leads.append(lax.ppermute(lead, ("cone", "con"), pairs))
    lead = call(
        functools.partial(pick_lead_kernel, owners),
        shaped(coded_square, row_dev, I16),
        tuple(leads),
        limit=4,
    )
    rest_own, *rest_codes = call(
        functools.partial(sum_rest_kernel, owners, cones),
        terms_shape,
        (jnp.array(order, jnp.int32), *[part for group in summed for part in group]),
        [pltpu.VMEM((cones, share, per_block), F32)],
        16,
        1,
    )
    rest_codes = exchange(rest_codes, lambda u: [(i, i ^ u) for i in range(cones) if i ^ u])
    factor_rows, row_factor = call(
        rows_kernel,
        (shaped(PANEL, per_block, F32), shaped(PANEL, PANEL, F32)),
        (inverse, panel, *beside(lead)),
        [pltpu.VMEM((PANEL, PANEL), F32)],
        14,
    )
    return call(
        functools.partial(update_kernel, owners, row_dev),
        shaped(PANEL, per_block, F32),
        (factor_rows, row_factor, rest_own, *rest_codes),
        limit=14,
    )


def solution(mesh):
    in_specs = (
        P("cone", "con", None),
        P("cone", None, None),
        P("cone", None, None),
        P("cone", None),
    )
    out_specs = P("cone", "con")

    return jax.shard_map(shards, mesh=mesh, in_specs=in_specs, out_specs=out_specs, check_vma=False)
```

profile of v0, /device:TPU:21, one launch (start us, length us, event | category | flops | bytes accessed | tf_op | source)
XLA Modules:
  0.0 165.6 jit_solution(16597398849543763795)
XLA Ops:
  0.0 0.7 copy-done.3
  0.7 1.3 mask_rows.1.refs_0_
  1.9 0.0 copy-start
  1.9 0.0 copy-start.4
  1.9 1.4 collective-permute-start.11
  3.3 1.9 %collective-permute-start.17 = (bf16[256,1024]{1,0:T(8,128)(2,1)S(1)}, bf16[256,1024]{1,0:T(8,128)(2,1)S(1)}, u32[]{:S(2)}, u32[]{:S(2)}) collective-permute-start(bf16[256,1024]{1,0:T(8,128)(2,1)S(1)} %mask_rows.1.refs_0_), channel_id=1, source_target_pairs={{2,4},{3,5},{4,2},{5,3},{10,12},{11,13},{12,10},{13,11},{18,20},{1... | collective-permute-start | bytes 1572872 | tf_op jit(solution)/shard_map/ppermute | solution.py:435
  5.2 0.7 collective-permute-start.16
  5.9 8.9 %collective-permute-done.11.refs_0_ = bf16[256,1024]{1,0:T(8,128)(2,1)S(1)} collective-permute-done((bf16[256,1024]{1,0:T(8,128)(2,1)S(1)}, bf16[256,1024]{1,0:T(8,128)(2,1)S(1)}, u32[]{:S(2)}, u32[]{:S(2)}) %collective-permute-start.11) | collective-permute-done | bytes 524320 | tf_op jit(solution)/shard_map/ppermute | solution.py:435
  14.8 2.1 %collective-permute-start.18 = (bf16[256,1024]{1,0:T(8,128)(2,1)S(1)}, bf16[256,1024]{1,0:T(8,128)(2,1)S(1)}, u32[]{:S(2)}, u32[]{:S(2)}) collective-permute-start(bf16[256,1024]{1,0:T(8,128)(2,1)S(1)} %collective-permute-done.11.refs_0_), channel_id=1, source_target_pairs={{2,4},{3,5},{4,2},{5,3},{10,12},{11,13},{12,10},{13,11},{18,20},{1... | collective-permute-start | bytes 1572872 | tf_op jit(solution)/shard_map/ppermute | solution.py:435
  16.9 3.0 %collective-permute-start = (bf16[256,1024]{1,0:T(8,128)(2,1)S(1)}, bf16[256,1024]{1,0:T(8,128)(2,1)S(1)}, u32[]{:S(2)}, u32[]{:S(2)}) collective-permute-start(bf16[256,1024]{1,0:T(8,128)(2,1)S(1)} %mask_rows.1.refs_0_), channel_id=1, source_target_pairs={{0,1},{1,0},{2,3},{3,2},{4,5},{5,4},{6,7},{7,6},{8,9},{9,8},{10,11... | collective-permute-start | bytes 1572872 | tf_op jit(solution)/shard_map/ppermute | solution.py:445
  19.9 0.1 collective-permute-start.12
  20.0 8.9 %collective-permute-done.17.refs_1_.refs_0_ = bf16[256,1024]{1,0:T(8,128)(2,1)S(1)} collective-permute-done((bf16[256,1024]{1,0:T(8,128)(2,1)S(1)}, bf16[256,1024]{1,0:T(8,128)(2,1)S(1)}, u32[]{:S(2)}, u32[]{:S(2)}) %collective-permute-start.17) | collective-permute-done | bytes 524320 | tf_op jit(solution)/shard_map/ppermute | solution.py:435
  29.0 11.2 %collective-permute-done.18.refs_2_ = bf16[256,1024]{1,0:T(8,128)(2,1)S(1)} collective-permute-done((bf16[256,1024]{1,0:T(8,128)(2,1)S(1)}, bf16[256,1024]{1,0:T(8,128)(2,1)S(1)}, u32[]{:S(2)}, u32[]{:S(2)}) %collective-permute-start.18) | collective-permute-done | bytes 524320 | tf_op jit(solution)/shard_map/ppermute | solution.py:435
  40.2 1.9 %collective-permute-start.19 = (bf16[256,1024]{1,0:T(8,128)(2,1)S(1)}, bf16[256,1024]{1,0:T(8,128)(2,1)S(1)}, u32[]{:S(2)}, u32[]{:S(2)}) collective-permute-start(bf16[256,1024]{1,0:T(8,128)(2,1)S(1)} %shard_map.63.refs_0_), channel_id=1, source_target_pairs={{0,1},{1,0},{2,3},{3,2},{4,5},{5,4},{6,7},{7,6},{8,9},{9,8},{10,11... | collective-permute-start | bytes 1572872 | tf_op jit(solution)/shard_map/ppermute | solution.py:445
  42.1 6.1 %shard_map.55 = (f32[128,1024]{1,0:T(8,128)S(1)}, s16[136,1024]{1,0:T(8,128)(2,1)S(1)}, s16[136,1024]{1,0:T(8,128)(2,1)S(1)}, s16[136,1024]{1,0:T(8,128)(2,1)S(1...) custom-call(s32[1,8]{1,0:T(1,128)S(1)} %copy-done.4, bf16[256,1024]{1,0:T(8,128)(2,1)S(1)} %mask_rows.1.refs_0_, ...), custom_call_target="tpu_custom_call" | custom-call | tf_op jit(solution)/shard_map/pallas_call | solution.py:374
  48.3 1.3 collective-permute-start.8
  49.5 0.2 collective-permute-start.9
  49.8 1.3 collective-permute-start.30
  51.1 0.0 collective-permute-done.12.refs_1_
  51.1 1.3 collective-permute-start.10
  52.4 6.0 %shard_map.62 = (f32[128,1024]{1,0:T(8,128)S(1)}, s16[136,1024]{1,0:T(8,128)(2,1)S(1)}, s16[136,1024]{1,0:T(8,128)(2,1)S(1)}, s16[136,1024]{1,0:T(8,128)(2,1)S(1)}) custom-call(s32[1,8]{1,0:T(1,128)S(1)} %copy-done.4, bf16[256,1024]{1,0:T(8,128)(2,1)S(1)} %shard_map.61.refs_0_, bf16[256,1024]{1,0:T(8,128)(2,1)S(1)} %collective-permute-done.12.refs_1_, ...), custom_call_target="tpu_custom_call" | custom-call | tf_op jit(solution)/shard_map/pallas_call | solution.py:374
  58.4 0.0 collective-permute-done.8.refs_1_
  58.4 1.3 collective-permute-start.13
  59.7 3.6 %collective-permute-done.9.refs_2_ = s16[136,1024]{1,0:T(8,128)(2,1)S(1)} collective-permute-done((s16[136,1024]{1,0:T(8,128)(2,1)S(1)}, s16[136,1024]{1,0:T(8,128)(2,1)S(1)}, u32[]{:S(2)}, u32[]{:S(2)}) %collective-permute-start.9) | collective-permute-done | bytes 278560 | tf_op jit(solution)/shard_map/ppermute | solution.py:431
  63.3 0.0 collective-permute-start.14
  63.3 0.0 collective-permute-done.19.refs_1_
  63.3 6.0 %shard_map.64 = (f32[128,1024]{1,0:T(8,128)S(1)}, s16[136,1024]{1,0:T(8,128)(2,1)S(1)}, s16[136,1024]{1,0:T(8,128)(2,1)S(1)}, s16[136,1024]{1,0:T(8,128)(2,1)S(1)}) custom-call(s32[1,8]{1,0:T(1,128)S(1)} %copy-done.4, bf16[256,1024]{1,0:T(8,128)(2,1)S(1)} %shard_map.63.refs_0_, bf16[256,1024]{1,0:T(8,128)(2,1)S(1)} %collective-permute-done.19.refs_1_, ...), custom_call_target="tpu_custom_call" | custom-call | tf_op jit(solution)/shard_map/pallas_call | solution.py:374
  69.4 2.7 %collective-permute-start.20 = (s16[136,1024]{1,0:T(8,128)(2,1)S(1)}, s16[136,1024]{1,0:T(8,128)(2,1)S(1)}, u32[]{:S(2)}, u32[]{:S(2)}) collective-permute-start(s16[136,1024]{1,0:T(8,128)(2,1)S(1)} %get-tuple-element.54), channel_id=1, source_target_pairs={{0,8},{8,0},{16,24},{24,16},{1,9},{9,1},{17,25},{25,17},{2,10},{10... | collective-permute-start | bytes 835592 | tf_op jit(solution)/shard_map/ppermute | solution.py:431
  72.1 1.3 collective-permute-start.22
  73.4 2.9 %collective-permute-done.14.refs_6_ = s16[136,1024]{1,0:T(8,128)(2,1)S(1)} collective-permute-done((s16[136,1024]{1,0:T(8,128)(2,1)S(1)}, s16[136,1024]{1,0:T(8,128)(2,1)S(1)}, u32[]{:S(2)}, u32[]{:S(2)}) %collective-permute-start.14) | collective-permute-done | bytes 278560 | tf_op jit(solution)/shard_map/ppermute | solution.py:431
  76.3 0.7 collective-permute-start.3
  76.9 0.1 shard_map.69.refs_0_
  77.0 3.9 %collective-permute-start.31 = (bf16[256,1024]{1,0:T(8,128)(2,1)S(1)}, bf16[256,1024]{1,0:T(8,128)(2,1)S(1)}, u32[]{:S(2)}, u32[]{:S(2)}) collective-permute-start(bf16[256,1024]{1,0:T(8,128)(2,1)S(1)} %shard_map.69.refs_0_), channel_id=1, source_target_pairs={{0,1},{1,0},{2,3},{3,2},{4,5},{5,4},{6,7},{7,6},{8,9},{9,8},{10,11... | collective-permute-start | bytes 1572872 | tf_op jit(solution)/shard_map/ppermute | solution.py:445
  80.9 0.8 collective-permute-start.2
  81.8 6.4 %collective-permute-done.21.refs_10_ = s16[136,1024]{1,0:T(8,128)(2,1)S(1)} collective-permute-done((s16[136,1024]{1,0:T(8,128)(2,1)S(1)}, s16[136,1024]{1,0:T(8,128)(2,1)S(1)}, u32[]{:S(2)}, u32[]{:S(2)}) %collective-permute-start.21) | collective-permute-done | bytes 278560 | tf_op jit(solution)/shard_map/ppermute | solution.py:431
  88.2 0.7 collective-permute-start.1
  88.9 0.4 shard_map.65
  89.3 0.1 collective-permute-start.25
  89.4 0.1 collective-permute-start.24
  89.5 2.5 %collective-permute-start.23 = (s16[136,1024]{1,0:T(8,128)(2,1)S(1)}, s16[136,1024]{1,0:T(8,128)(2,1)S(1)}, u32[]{:S(2)}, u32[]{:S(2)}) collective-permute-start(s16[136,1024]{1,0:T(8,128)(2,1)S(1)} %get-tuple-element.58), channel_id=1, source_target_pairs={{0,8},{8,0},{16,24},{24,16},{1,9},{9,1},{17,25},{25,17},{2,10},{10... | collective-permute-start | bytes 835592 | tf_op jit(solution)/shard_map/ppermute | solution.py:431
  92.0 0.4 shard_map.56.refs_0_
  92.4 0.7 collective-permute-start.6
  93.1 1.3 collective-permute-start.5
  94.4 6.0 %shard_map.70 = (f32[128,1024]{1,0:T(8,128)S(1)}, s16[136,1024]{1,0:T(8,128)(2,1)S(1)}, s16[136,1024]{1,0:T(8,128)(2,1)S(1)}, s16[136,1024]{1,0:T(8,128)(2,1)S(1)}) custom-call(s32[1,8]{1,0:T(1,128)S(1)} %copy-done.4, bf16[256,1024]{1,0:T(8,128)(2,1)S(1)} %shard_map.69.refs_0_, bf16[256,1024]{1,0:T(8,128)(2,1)S(1)} %collective-permute-done.31.refs_1_, ...), custom_call_target="tpu_custom_call" | custom-call | tf_op jit(solution)/shard_map/pallas_call | solution.py:374
  100.4 0.0 copy-start.5
  100.4 0.7 collective-permute-start.4
  101.1 2.1 %collective-permute-done.24.refs_1_ = s16[136,1024]{1,0:T(8,128)(2,1)S(1)} collective-permute-done((s16[136,1024]{1,0:T(8,128)(2,1)S(1)}, s16[136,1024]{1,0:T(8,128)(2,1)S(1)}, u32[]{:S(2)}, u32[]{:S(2)}) %collective-permute-start.24) | collective-permute-done | bytes 278560 | tf_op jit(solution)/shard_map/ppermute | solution.py:431
  103.2 1.7 %collective-permute-start.33 = (s16[136,1024]{1,0:T(8,128)(2,1)S(1)}, s16[136,1024]{1,0:T(8,128)(2,1)S(1)}, u32[]{:S(2)}, u32[]{:S(2)}) collective-permute-start(s16[136,1024]{1,0:T(8,128)(2,1)S(1)} %get-tuple-element.65), channel_id=1, source_target_pairs={{0,16},{8,24},{16,0},{24,8},{1,17},{9,25},{17,1},{25,9},{2,18},{10... | collective-permute-start | bytes 835592 | tf_op jit(solution)/shard_map/ppermute | solution.py:431
  104.8 0.4 shard_map.66
  105.3 1.0 collective-permute-start.34
  106.3 1.9 %collective-permute-start.28 = (s16[544,256]{1,0:T(8,128)(2,1)S(1)}, s16[544,256]{1,0:T(8,128)(2,1)S(1)}, u32[]{:S(2)}, u32[]{:S(2)}) collective-permute-start(s16[544,256]{1,0:T(8,128)(2,1)S(1)} %get-tuple-element.60.refs_0_), channel_id=1, source_target_pairs={{10,12},{11,13},{20,18},{21,19},{30,24},{31,25}} | collective-permute-start | bytes 835592 | tf_op jit(solution)/shard_map/ppermute | solution.py:553
  108.3 4.1 %collective-permute-start.27 = (s16[544,256]{1,0:T(8,128)(2,1)S(1)}, s16[544,256]{1,0:T(8,128)(2,1)S(1)}, u32[]{:S(2)}, u32[]{:S(2)}) collective-permute-start(s16[544,256]{1,0:T(8,128)(2,1)S(1)} %get-tuple-element.60.refs_0_), channel_id=1, source_target_pairs={{10,14},{11,15},{20,16},{21,17},{30,26},{31,27}} | collective-permute-start | bytes 835592 | tf_op jit(solution)/shard_map/ppermute | solution.py:553
  112.4 1.3 collective-permute-start.26
  113.8 3.9 %collective-permute-start.7 = (s16[544,256]{1,0:T(8,128)(2,1)S(1)}, s16[544,256]{1,0:T(8,128)(2,1)S(1)}, u32[]{:S(2)}, u32[]{:S(2)}) collective-permute-start(s16[544,256]{1,0:T(8,128)(2,1)S(1)} %shard_map.57.refs_0_), channel_id=1, source_target_pairs={{0,1},{1,0},{2,3},{3,2},{4,5},{5,4},{6,7},{7,6},{8,9},{9,8},{10,11... | collective-permute-start | bytes 835592 | tf_op jit(solution)/shard_map/ppermute | solution.py:445
  117.7 1.6 shard_map.71
  119.4 1.8 %collective-permute-start.29 = (s16[544,256]{1,0:T(8,128)(2,1)S(1)}, s16[544,256]{1,0:T(8,128)(2,1)S(1)}, u32[]{:S(2)}, u32[]{:S(2)}) collective-permute-start(s16[544,256]{1,0:T(8,128)(2,1)S(1)} %shard_map.67.refs_0_), channel_id=1, source_target_pairs={{0,1},{1,0},{2,3},{3,2},{4,5},{5,4},{6,7},{7,6},{8,9},{9,8},{10,11... | collective-permute-start | bytes 835592 | tf_op jit(solution)/shard_map/ppermute | solution.py:445
  121.2 11.7 %collective-permute-start.35 = (s16[136,1024]{1,0:T(8,128)(2,1)S(1)}, s16[136,1024]{1,0:T(8,128)(2,1)S(1)}, u32[]{:S(2)}, u32[]{:S(2)}) collective-permute-start(s16[136,1024]{1,0:T(8,128)(2,1)S(1)} %get-tuple-element.68), channel_id=1, source_target_pairs={{0,8},{16,24},{24,16},{1,9},{17,25},{25,17},{2,10},{18,26},{26,18}... | collective-permute-start | bytes 835592 | tf_op jit(solution)/shard_map/ppermute | solution.py:431
  132.9 1.3 collective-permute-start.36
  134.2 3.9 %collective-permute-start.37 = (s16[136,1024]{1,0:T(8,128)(2,1)S(1)}, s16[136,1024]{1,0:T(8,128)(2,1)S(1)}, u32[]{:S(2)}, u32[]{:S(2)}) collective-permute-start(s16[136,1024]{1,0:T(8,128)(2,1)S(1)} %get-tuple-element.70), channel_id=1, source_target_pairs={{0,24},{8,16},{16,8},{1,25},{9,17},{17,9},{2,26},{10,18},{18,10},{... | collective-permute-start | bytes 835592 | tf_op jit(solution)/shard_map/ppermute | solution.py:431
  138.2 0.7 shard_map.58
  138.8 11.6 %shard_map.59 = (f32[512,512]{1,0:T(8,128)S(1)}, f32[512,512]{1,0:T(8,128)S(1)}) custom-call(f32[512,512]{1,0:T(8,128)S(1)} %get-tuple-element.40.work_in, f32[512,512]{1,0:T(8,128)S(1)} %get-tuple-element.41.x_in), custom_call_target="tpu_custom_call", output_to_operand_aliasing={{0}: (0, {}), {1}: (1, {})} | custom-call | tf_op jit(solution)/shard_map/pallas_call | solution.py:132
  150.4 9.1 %shard_map.60 = (f32[512,512]{1,0:T(8,128)S(1)}, f32[512,512]{1,0:T(8,128)S(1)}) custom-call(f32[512,512]{1,0:T(8,128)S(1)} %get-tuple-element.42.work_in, f32[512,512]{1,0:T(8,128)S(1)} %get-tuple-element.43.x_in), custom_call_target="tpu_custom_call", output_to_operand_aliasing={{0}: (0, {}), {1}: (1, {})} | custom-call | tf_op jit(solution)/shard_map/pallas_call | solution.py:132
  159.5 2.7 %shard_map.68 = (f32[512,1024]{1,0:T(8,128)S(1)}, f32[512,512]{1,0:T(8,128)S(1)}) custom-call(f32[512,512]{1,0:T(8,128)S(1)} %get-tuple-element.44.inverse_ref, f32[512,1024]{1,0:T(8,128)S(1)} %get-tuple-element.59.panel_ref, s16[544,256]{1,0:T(8,128)(2,1)S(1)} %shard_map.67.refs_0_, s16[544,256]{1,0:T(8,128)(2,1)S(1)} %collective-permute-done.29.refs_1_), custom_call_target="tpu_custom_call" | custom-call | tf_op jit(solution)/shard_map/pallas_call | solution.py:374
  162.3 3.4 %shard_map.72 = f32[512,1024]{1,0:T(8,128)} custom-call(f32[512,1024]{1,0:T(8,128)S(1)} %get-tuple-element.61.factor_ref, f32[512,512]{1,0:T(8,128)S(1)} %get-tuple-element.62.row_ref, f32[128,1024]{1,0:T(8,128)S(1)} %get-tuple-element.67.own_ref, s16[136,1024]{1,0:T(8,128)(2,1)S(1)} %collective-permute-done.35.refs_0_, ...), custom_call_target="tpu_custom_call" | custom-call | tf_op jit(solution)/shard_map/pallas_call | solution.py:374
  (43 shorter events, 0.3 us)
Async XLA Ops:
  0.0 0.7 copy-start.3
  0.7 41.5 %copy-start.1 = (bf16[1,1024,1024]{2,1,0:T(8,128)(2,1)S(1)}, bf16[1,1024,1024]{2,1,0:T(8,128)(2,1)}, u32[]{:S(2)}) copy-start(bf16[1,1024,1024]{2,1,0:T(8,128)(2,1)} %param.6) | copy-start | bytes 6291460
  0.7 41.5 %copy-start.2 = (bf16[1,1024,1024]{2,1,0:T(8,128)(2,1)S(1)}, bf16[1,1024,1024]{2,1,0:T(8,128)(2,1)}, u32[]{:S(2)}) copy-start(bf16[1,1024,1024]{2,1,0:T(8,128)(2,1)} %param.7) | copy-start | bytes 6291460
  1.9 40.2 %copy-start = (bf16[1,1024,1024]{2,1,0:T(8,128)(2,1)S(1)}, bf16[1,1024,1024]{2,1,0:T(8,128)(2,1)}, u32[]{:S(2)}) copy-start(bf16[1,1024,1024]{2,1,0:T(8,128)(2,1)} %param.5) | copy-start | bytes 6291460
  1.9 40.2 %copy-start.4 = (s32[1,8]{1,0:T(1,128)S(1)}, s32[1,8]{1,0:T(1,128)}, u32[]{:S(2)}) copy-start(s32[1,8]{1,0:T(1,128)} %touches_ref.9) | copy-start | bytes 100
  1.9 12.9 %collective-permute-start.11 = (bf16[256,1024]{1,0:T(8,128)(2,1)S(1)}, bf16[256,1024]{1,0:T(8,128)(2,1)S(1)}, u32[]{:S(2)}, u32[]{:S(2)}) collective-permute-start(bf16[256,1024]{1,0:T(8,128)(2,1)S(1)} %mask_rows.1.refs_0_), channel_id=1, source_target_pairs={{0,2},{1,3},{2,0},{3,1},{4,6},{5,7},{6,4},{7,5},{8,10},{9,11},{10,... | collective-permute-start | bytes 1572872 | tf_op jit(solution)/shard_map/ppermute | solution.py:435
  3.3 25.6 %collective-permute-start.17 = (bf16[256,1024]{1,0:T(8,128)(2,1)S(1)}, bf16[256,1024]{1,0:T(8,128)(2,1)S(1)}, u32[]{:S(2)}, u32[]{:S(2)}) collective-permute-start(bf16[256,1024]{1,0:T(8,128)(2,1)S(1)} %mask_rows.1.refs_0_), channel_id=1, source_target_pairs={{2,4},{3,5},{4,2},{5,3},{10,12},{11,13},{12,10},{13,11},{18,20},{1... | collective-permute-start | bytes 1572872 | tf_op jit(solution)/shard_map/ppermute | solution.py:435
  5.2 23.7 %collective-permute-start.16 = (bf16[256,1024]{1,0:T(8,128)(2,1)S(1)}, bf16[256,1024]{1,0:T(8,128)(2,1)S(1)}, u32[]{:S(2)}, u32[]{:S(2)}) collective-permute-start(bf16[256,1024]{1,0:T(8,128)(2,1)S(1)} %mask_rows.1.refs_0_), channel_id=1, source_target_pairs={{0,6},{1,7},{6,0},{7,1},{8,14},{9,15},{14,8},{15,9},{16,22},{17,23... | collective-permute-start | bytes 1572872 | tf_op jit(solution)/shard_map/ppermute | solution.py:435
  14.8 25.4 %collective-permute-start.18 = (bf16[256,1024]{1,0:T(8,128)(2,1)S(1)}, bf16[256,1024]{1,0:T(8,128)(2,1)S(1)}, u32[]{:S(2)}, u32[]{:S(2)}) collective-permute-start(bf16[256,1024]{1,0:T(8,128)(2,1)S(1)} %collective-permute-done.11.refs_0_), channel_id=1, source_target_pairs={{2,4},{3,5},{4,2},{5,3},{10,12},{11,13},{12,10},{13,11},{18,20},{1... | collective-permute-start | bytes 1572872 | tf_op jit(solution)/shard_map/ppermute | solution.py:435
  16.9 25.2 %collective-permute-start = (bf16[256,1024]{1,0:T(8,128)(2,1)S(1)}, bf16[256,1024]{1,0:T(8,128)(2,1)S(1)}, u32[]{:S(2)}, u32[]{:S(2)}) collective-permute-start(bf16[256,1024]{1,0:T(8,128)(2,1)S(1)} %mask_rows.1.refs_0_), channel_id=1, source_target_pairs={{0,1},{1,0},{2,3},{3,2},{4,5},{5,4},{6,7},{7,6},{8,9},{9,8},{10,11... | collective-permute-start | bytes 1572872 | tf_op jit(solution)/shard_map/ppermute | solution.py:445
  19.9 31.2 %collective-permute-start.12 = (bf16[256,1024]{1,0:T(8,128)(2,1)S(1)}, bf16[256,1024]{1,0:T(8,128)(2,1)S(1)}, u32[]{:S(2)}, u32[]{:S(2)}) collective-permute-start(bf16[256,1024]{1,0:T(8,128)(2,1)S(1)} %shard_map.61.refs_0_), channel_id=1, source_target_pairs={{0,1},{1,0},{2,3},{3,2},{4,5},{5,4},{6,7},{7,6},{8,9},{9,8},{10,11... | collective-permute-start | bytes 1572872 | tf_op jit(solution)/shard_map/ppermute | solution.py:445
  40.2 23.1 %collective-permute-start.19 = (bf16[256,1024]{1,0:T(8,128)(2,1)S(1)}, bf16[256,1024]{1,0:T(8,128)(2,1)S(1)}, u32[]{:S(2)}, u32[]{:S(2)}) collective-permute-start(bf16[256,1024]{1,0:T(8,128)(2,1)S(1)} %shard_map.63.refs_0_), channel_id=1, source_target_pairs={{0,1},{1,0},{2,3},{3,2},{4,5},{5,4},{6,7},{7,6},{8,9},{9,8},{10,11... | collective-permute-start | bytes 1572872 | tf_op jit(solution)/shard_map/ppermute | solution.py:445
  48.3 10.1 %collective-permute-start.8 = (s16[136,1024]{1,0:T(8,128)(2,1)S(1)}, s16[136,1024]{1,0:T(8,128)(2,1)S(1)}, u32[]{:S(2)}, u32[]{:S(2)}) collective-permute-start(s16[136,1024]{1,0:T(8,128)(2,1)S(1)} %get-tuple-element.46), channel_id=1, source_target_pairs={{0,8},{8,0},{16,24},{24,16},{1,9},{9,1},{17,25},{25,17},{2,10},{10... | collective-permute-start | bytes 835592 | tf_op jit(solution)/shard_map/ppermute | solution.py:431
  49.5 13.8 %collective-permute-start.9 = (s16[136,1024]{1,0:T(8,128)(2,1)S(1)}, s16[136,1024]{1,0:T(8,128)(2,1)S(1)}, u32[]{:S(2)}, u32[]{:S(2)}) collective-permute-start(s16[136,1024]{1,0:T(8,128)(2,1)S(1)} %get-tuple-element.47), channel_id=1, source_target_pairs={{0,16},{8,24},{16,0},{24,8},{1,17},{9,25},{17,1},{25,9},{2,18},{10... | collective-permute-start | bytes 835592 | tf_op jit(solution)/shard_map/ppermute | solution.py:431
  49.8 22.3 %collective-permute-start.30 = (bf16[256,1024]{1,0:T(8,128)(2,1)S(1)}, bf16[256,1024]{1,0:T(8,128)(2,1)S(1)}, u32[]{:S(2)}, u32[]{:S(2)}) collective-permute-start(bf16[256,1024]{1,0:T(8,128)(2,1)S(1)} %collective-permute-done.17.refs_1_.refs_0_), channel_id=1, source_target_pairs={{2,0},{3,1},{4,6},{5,7},{10,8},{11,9},{12,14},{13,15},{18,16},{19,... | collective-permute-start | bytes 1572872 | tf_op jit(solution)/shard_map/ppermute | solution.py:435
  51.1 18.2 %collective-permute-start.10 = (s16[136,1024]{1,0:T(8,128)(2,1)S(1)}, s16[136,1024]{1,0:T(8,128)(2,1)S(1)}, u32[]{:S(2)}, u32[]{:S(2)}) collective-permute-start(s16[136,1024]{1,0:T(8,128)(2,1)S(1)} %get-tuple-element.48), channel_id=1, source_target_pairs={{0,24},{8,16},{16,8},{24,0},{1,25},{9,17},{17,9},{25,1},{2,26},{10... | collective-permute-start | bytes 835592 | tf_op jit(solution)/shard_map/ppermute | solution.py:431
  58.4 13.7 %collective-permute-start.13 = (s16[136,1024]{1,0:T(8,128)(2,1)S(1)}, s16[136,1024]{1,0:T(8,128)(2,1)S(1)}, u32[]{:S(2)}, u32[]{:S(2)}) collective-permute-start(s16[136,1024]{1,0:T(8,128)(2,1)S(1)} %get-tuple-element.50), channel_id=1, source_target_pairs={{0,8},{8,0},{16,24},{24,16},{1,9},{9,1},{17,25},{25,17},{2,10},{10... | collective-permute-start | bytes 835592 | tf_op jit(solution)/shard_map/ppermute | solution.py:431
  63.3 12.9 %collective-permute-start.14 = (s16[136,1024]{1,0:T(8,128)(2,1)S(1)}, s16[136,1024]{1,0:T(8,128)(2,1)S(1)}, u32[]{:S(2)}, u32[]{:S(2)}) collective-permute-start(s16[136,1024]{1,0:T(8,128)(2,1)S(1)} %get-tuple-element.51), channel_id=1, source_target_pairs={{0,16},{8,24},{16,0},{24,8},{1,17},{9,25},{17,1},{25,9},{2,18},{10... | collective-permute-start | bytes 835592 | tf_op jit(solution)/shard_map/ppermute | solution.py:431
  63.3 13.7 %collective-permute-start.15 = (s16[136,1024]{1,0:T(8,128)(2,1)S(1)}, s16[136,1024]{1,0:T(8,128)(2,1)S(1)}, u32[]{:S(2)}, u32[]{:S(2)}) collective-permute-start(s16[136,1024]{1,0:T(8,128)(2,1)S(1)} %get-tuple-element.52), channel_id=1, source_target_pairs={{0,24},{8,16},{16,8},{24,0},{1,25},{9,17},{17,9},{25,1},{2,26},{10... | collective-permute-start | bytes 835592 | tf_op jit(solution)/shard_map/ppermute | solution.py:431
  69.4 11.5 %collective-permute-start.20 = (s16[136,1024]{1,0:T(8,128)(2,1)S(1)}, s16[136,1024]{1,0:T(8,128)(2,1)S(1)}, u32[]{:S(2)}, u32[]{:S(2)}) collective-permute-start(s16[136,1024]{1,0:T(8,128)(2,1)S(1)} %get-tuple-element.54), channel_id=1, source_target_pairs={{0,8},{8,0},{16,24},{24,16},{1,9},{9,1},{17,25},{25,17},{2,10},{10... | collective-permute-start | bytes 835592 | tf_op jit(solution)/shard_map/ppermute | solution.py:431
  72.1 16.1 %collective-permute-start.21 = (s16[136,1024]{1,0:T(8,128)(2,1)S(1)}, s16[136,1024]{1,0:T(8,128)(2,1)S(1)}, u32[]{:S(2)}, u32[]{:S(2)}) collective-permute-start(s16[136,1024]{1,0:T(8,128)(2,1)S(1)} %get-tuple-element.55), channel_id=1, source_target_pairs={{0,16},{8,24},{16,0},{24,8},{1,17},{9,25},{17,1},{25,9},{2,18},{10... | collective-permute-start | bytes 835592 | tf_op jit(solution)/shard_map/ppermute | solution.py:431
  72.1 16.8 %collective-permute-start.22 = (s16[136,1024]{1,0:T(8,128)(2,1)S(1)}, s16[136,1024]{1,0:T(8,128)(2,1)S(1)}, u32[]{:S(2)}, u32[]{:S(2)}) collective-permute-start(s16[136,1024]{1,0:T(8,128)(2,1)S(1)} %get-tuple-element.56), channel_id=1, source_target_pairs={{0,24},{8,16},{16,8},{24,0},{1,25},{9,17},{17,9},{25,1},{2,26},{10... | collective-permute-start | bytes 835592 | tf_op jit(solution)/shard_map/ppermute | solution.py:431
  76.3 13.1 %collective-permute-start.3 = (s16[544,256]{1,0:T(8,128)(2,1)S(1)}, s16[544,256]{1,0:T(8,128)(2,1)S(1)}, u32[]{:S(2)}, u32[]{:S(2)}) collective-permute-start(s16[544,256]{1,0:T(8,128)(2,1)S(1)} %get-tuple-element.39), channel_id=1, source_target_pairs={{0,24},{1,25},{8,16},{9,17},{16,8},{17,9},{24,0},{25,1}} | collective-permute-start | bytes 835592 | tf_op jit(solution)/shard_map/ppermute | solution.py:506
  77.0 16.0 %collective-permute-start.31 = (bf16[256,1024]{1,0:T(8,128)(2,1)S(1)}, bf16[256,1024]{1,0:T(8,128)(2,1)S(1)}, u32[]{:S(2)}, u32[]{:S(2)}) collective-permute-start(bf16[256,1024]{1,0:T(8,128)(2,1)S(1)} %shard_map.69.refs_0_), channel_id=1, source_target_pairs={{0,1},{1,0},{2,3},{3,2},{4,5},{5,4},{6,7},{7,6},{8,9},{9,8},{10,11... | collective-permute-start | bytes 1572872 | tf_op jit(solution)/shard_map/ppermute | solution.py:445
  80.9 8.5 %collective-permute-start.2 = (s16[544,256]{1,0:T(8,128)(2,1)S(1)}, s16[544,256]{1,0:T(8,128)(2,1)S(1)}, u32[]{:S(2)}, u32[]{:S(2)}) collective-permute-start(s16[544,256]{1,0:T(8,128)(2,1)S(1)} %get-tuple-element.39), channel_id=1, source_target_pairs={{0,16},{1,17},{8,24},{9,25},{16,0},{17,1},{24,8},{25,9}} | collective-permute-start | bytes 835592 | tf_op jit(solution)/shard_map/ppermute | solution.py:506
  88.2 3.8 %collective-permute-start.1 = (s16[544,256]{1,0:T(8,128)(2,1)S(1)}, s16[544,256]{1,0:T(8,128)(2,1)S(1)}, u32[]{:S(2)}, u32[]{:S(2)}) collective-permute-start(s16[544,256]{1,0:T(8,128)(2,1)S(1)} %get-tuple-element.39), channel_id=1, source_target_pairs={{0,8},{1,9},{8,0},{9,1},{16,24},{17,25},{24,16},{25,17}} | collective-permute-start | bytes 835592 | tf_op jit(solution)/shard_map/ppermute | solution.py:506
  89.3 11.1 %collective-permute-start.25 = (s16[136,1024]{1,0:T(8,128)(2,1)S(1)}, s16[136,1024]{1,0:T(8,128)(2,1)S(1)}, u32[]{:S(2)}, u32[]{:S(2)}) collective-permute-start(s16[136,1024]{1,0:T(8,128)(2,1)S(1)} %get-tuple-element.58), channel_id=1, source_target_pairs={{0,24},{8,16},{16,8},{24,0},{1,25},{9,17},{17,9},{25,1},{2,26},{10... | collective-permute-start | bytes 835592 | tf_op jit(solution)/shard_map/ppermute | solution.py:431
  89.4 13.8 %collective-permute-start.24 = (s16[136,1024]{1,0:T(8,128)(2,1)S(1)}, s16[136,1024]{1,0:T(8,128)(2,1)S(1)}, u32[]{:S(2)}, u32[]{:S(2)}) collective-permute-start(s16[136,1024]{1,0:T(8,128)(2,1)S(1)} %get-tuple-element.58), channel_id=1, source_target_pairs={{0,16},{8,24},{16,0},{24,8},{1,17},{9,25},{17,1},{25,9},{2,18},{10... | collective-permute-start | bytes 835592 | tf_op jit(solution)/shard_map/ppermute | solution.py:431
  89.5 13.7 %collective-permute-start.23 = (s16[136,1024]{1,0:T(8,128)(2,1)S(1)}, s16[136,1024]{1,0:T(8,128)(2,1)S(1)}, u32[]{:S(2)}, u32[]{:S(2)}) collective-permute-start(s16[136,1024]{1,0:T(8,128)(2,1)S(1)} %get-tuple-element.58), channel_id=1, source_target_pairs={{0,8},{8,0},{16,24},{24,16},{1,9},{9,1},{17,25},{25,17},{2,10},{10... | collective-permute-start | bytes 835592 | tf_op jit(solution)/shard_map/ppermute | solution.py:431
  92.4 12.9 %collective-permute-start.6 = (s16[544,256]{1,0:T(8,128)(2,1)S(1)}, s16[544,256]{1,0:T(8,128)(2,1)S(1)}, u32[]{:S(2)}, u32[]{:S(2)}) collective-permute-start(s16[544,256]{1,0:T(8,128)(2,1)S(1)} %shard_map.56.refs_0_), channel_id=1, source_target_pairs={{0,6},{1,7},{8,14},{9,15},{16,22},{17,23},{24,30},{25,31}} | collective-permute-start | bytes 835592 | tf_op jit(solution)/shard_map/ppermute | solution.py:435
  93.1 13.3 %collective-permute-start.5 = (s16[544,256]{1,0:T(8,128)(2,1)S(1)}, s16[544,256]{1,0:T(8,128)(2,1)S(1)}, u32[]{:S(2)}, u32[]{:S(2)}) collective-permute-start(s16[544,256]{1,0:T(8,128)(2,1)S(1)} %shard_map.56.refs_0_), channel_id=1, source_target_pairs={{0,4},{1,5},{8,12},{9,13},{16,20},{17,21},{24,28},{25,29}} | collective-permute-start | bytes 835592 | tf_op jit(solution)/shard_map/ppermute | solution.py:435
  100.4 17.3 %copy-start.5 = (s32[4,4]{1,0:T(4,128)S(1)}, s32[4,4]{1,0:T(4,128)}, u32[]{:S(2)}) copy-start(s32[4,4]{1,0:T(4,128)} %constant.2.clone.order_ref) | copy-start | bytes 196
  100.4 7.9 %collective-permute-start.4 = (s16[544,256]{1,0:T(8,128)(2,1)S(1)}, s16[544,256]{1,0:T(8,128)(2,1)S(1)}, u32[]{:S(2)}, u32[]{:S(2)}) collective-permute-start(s16[544,256]{1,0:T(8,128)(2,1)S(1)} %shard_map.56.refs_0_), channel_id=1, source_target_pairs={{0,2},{1,3},{8,10},{9,11},{16,18},{17,19},{24,26},{25,27}} | collective-permute-start | bytes 835592 | tf_op jit(solution)/shard_map/ppermute | solution.py:435
  103.2 9.2 %collective-permute-start.32 = (s16[136,1024]{1,0:T(8,128)(2,1)S(1)}, s16[136,1024]{1,0:T(8,128)(2,1)S(1)}, u32[]{:S(2)}, u32[]{:S(2)}) collective-permute-start(s16[136,1024]{1,0:T(8,128)(2,1)S(1)} %get-tuple-element.64), channel_id=1, source_target_pairs={{0,8},{8,0},{16,24},{24,16},{1,9},{9,1},{17,25},{25,17},{2,10},{10... | collective-permute-start | bytes 835592 | tf_op jit(solution)/shard_map/ppermute | solution.py:431
  103.2 10.6 %collective-permute-start.33 = (s16[136,1024]{1,0:T(8,128)(2,1)S(1)}, s16[136,1024]{1,0:T(8,128)(2,1)S(1)}, u32[]{:S(2)}, u32[]{:S(2)}) collective-permute-start(s16[136,1024]{1,0:T(8,128)(2,1)S(1)} %get-tuple-element.65), channel_id=1, source_target_pairs={{0,16},{8,24},{16,0},{24,8},{1,17},{9,25},{17,1},{25,9},{2,18},{10... | collective-permute-start | bytes 835592 | tf_op jit(solution)/shard_map/ppermute | solution.py:431
  105.3 12.4 %collective-permute-start.34 = (s16[136,1024]{1,0:T(8,128)(2,1)S(1)}, s16[136,1024]{1,0:T(8,128)(2,1)S(1)}, u32[]{:S(2)}, u32[]{:S(2)}) collective-permute-start(s16[136,1024]{1,0:T(8,128)(2,1)S(1)} %get-tuple-element.66), channel_id=1, source_target_pairs={{0,24},{8,16},{16,8},{24,0},{1,25},{9,17},{17,9},{25,1},{2,26},{10... | collective-permute-start | bytes 835592 | tf_op jit(solution)/shard_map/ppermute | solution.py:431
  106.3 13.0 %collective-permute-start.28 = (s16[544,256]{1,0:T(8,128)(2,1)S(1)}, s16[544,256]{1,0:T(8,128)(2,1)S(1)}, u32[]{:S(2)}, u32[]{:S(2)}) collective-permute-start(s16[544,256]{1,0:T(8,128)(2,1)S(1)} %get-tuple-element.60.refs_0_), channel_id=1, source_target_pairs={{10,12},{11,13},{20,18},{21,19},{30,24},{31,25}} | collective-permute-start | bytes 835592 | tf_op jit(solution)/shard_map/ppermute | solution.py:553
  108.3 11.1 %collective-permute-start.27 = (s16[544,256]{1,0:T(8,128)(2,1)S(1)}, s16[544,256]{1,0:T(8,128)(2,1)S(1)}, u32[]{:S(2)}, u32[]{:S(2)}) collective-permute-start(s16[544,256]{1,0:T(8,128)(2,1)S(1)} %get-tuple-element.60.refs_0_), channel_id=1, source_target_pairs={{10,14},{11,15},{20,16},{21,17},{30,26},{31,27}} | collective-permute-start | bytes 835592 | tf_op jit(solution)/shard_map/ppermute | solution.py:553
  112.4 6.9 %collective-permute-start.26 = (s16[544,256]{1,0:T(8,128)(2,1)S(1)}, s16[544,256]{1,0:T(8,128)(2,1)S(1)}, u32[]{:S(2)}, u32[]{:S(2)}) collective-permute-start(s16[544,256]{1,0:T(8,128)(2,1)S(1)} %get-tuple-element.60.refs_0_), channel_id=1, source_target_pairs={{10,8},{11,9},{20,22},{21,23},{30,28},{31,29}} | collective-permute-start | bytes 835592 | tf_op jit(solution)/shard_map/ppermute | solution.py:553
  113.8 24.4 %collective-permute-start.7 = (s16[544,256]{1,0:T(8,128)(2,1)S(1)}, s16[544,256]{1,0:T(8,128)(2,1)S(1)}, u32[]{:S(2)}, u32[]{:S(2)}) collective-permute-start(s16[544,256]{1,0:T(8,128)(2,1)S(1)} %shard_map.57.refs_0_), channel_id=1, source_target_pairs={{0,1},{1,0},{2,3},{3,2},{4,5},{5,4},{6,7},{7,6},{8,9},{9,8},{10,11... | collective-permute-start | bytes 835592 | tf_op jit(solution)/shard_map/ppermute | solution.py:445
  119.4 40.1 %collective-permute-start.29 = (s16[544,256]{1,0:T(8,128)(2,1)S(1)}, s16[544,256]{1,0:T(8,128)(2,1)S(1)}, u32[]{:S(2)}, u32[]{:S(2)}) collective-permute-start(s16[544,256]{1,0:T(8,128)(2,1)S(1)} %shard_map.67.refs_0_), channel_id=1, source_target_pairs={{0,1},{1,0},{2,3},{3,2},{4,5},{5,4},{6,7},{7,6},{8,9},{9,8},{10,11... | collective-permute-start | bytes 835592 | tf_op jit(solution)/shard_map/ppermute | solution.py:445
  121.2 41.1 %collective-permute-start.35 = (s16[136,1024]{1,0:T(8,128)(2,1)S(1)}, s16[136,1024]{1,0:T(8,128)(2,1)S(1)}, u32[]{:S(2)}, u32[]{:S(2)}) collective-permute-start(s16[136,1024]{1,0:T(8,128)(2,1)S(1)} %get-tuple-element.68), channel_id=1, source_target_pairs={{0,8},{16,24},{24,16},{1,9},{17,25},{25,17},{2,10},{18,26},{26,18}... | collective-permute-start | bytes 835592 | tf_op jit(solution)/shard_map/ppermute | solution.py:431
  132.9 29.3 %collective-permute-start.36 = (s16[136,1024]{1,0:T(8,128)(2,1)S(1)}, s16[136,1024]{1,0:T(8,128)(2,1)S(1)}, u32[]{:S(2)}, u32[]{:S(2)}) collective-permute-start(s16[136,1024]{1,0:T(8,128)(2,1)S(1)} %get-tuple-element.69), channel_id=1, source_target_pairs={{0,16},{8,24},{24,8},{1,17},{9,25},{25,9},{2,18},{10,26},{26,10},{... | collective-permute-start | bytes 835592 | tf_op jit(solution)/shard_map/ppermute | solution.py:431
  134.2 28.1 %collective-permute-start.37 = (s16[136,1024]{1,0:T(8,128)(2,1)S(1)}, s16[136,1024]{1,0:T(8,128)(2,1)S(1)}, u32[]{:S(2)}, u32[]{:S(2)}) collective-permute-start(s16[136,1024]{1,0:T(8,128)(2,1)S(1)} %get-tuple-element.70), channel_id=1, source_target_pairs={{0,24},{8,16},{16,8},{1,25},{9,17},{17,9},{2,26},{10,18},{18,10},{... | collective-permute-start | bytes 835592 | tf_op jit(solution)/shard_map/ppermute | solution.py:431
where the time goes:
time: 166 us
  starting transfers between devices  64.4 us (39%)
  Pallas kernels  55.8 us (34%)
  waiting for transfers between devices  44.2 us (27%)
    pallas_call x16, Pallas kernels, call(): pl.pallas_call(kernel, out_shape=out_shape, in_specs=[in_smem()] * scalar...  33.9 us
    ppermute x18, starting transfers between devices, exchange(): lax.ppermute(code, 'cone', pairs(u))  30.3 us
    ppermute x8, waiting for transfers between devices, along(): return lax.ppermute(value, 'con', pairs)  29 us
    pallas_call x2, Pallas kernels, eliminate(): pl.pallas_call(functools.partial(eliminate_kernel, first, last), out_shap...  20.7 us
    ppermute x18, waiting for transfers between devices, exchange(): lax.ppermute(code, 'cone', pairs(u))  15.1 us
    ppermute x6, starting transfers between devices, beside(): swaps.append(lax.ppermute(value, 'con', pairs))  14.6 us
    ppermute x8, starting transfers between devices, along(): return lax.ppermute(value, 'con', pairs)  9.99 us
    ppermute x3, starting transfers between devices, shards(): leads.append(lax.ppermute(lead, ('cone', 'con'), pairs))  7.36 us
  transfers between devices with their start and end apart: 38, of which 7 were waited for; matrix products, arithmetic and copies ran while one was open for 0% of the time, Pallas kernels for 31%

commit v1 on v0

--- a/solution.py
+++ b/solution.py
@@ -15,7 +15,6 @@
 STEPS = 128
 LEVELS = 32767.0
 OCTAVE = math.log(2.0) / STEPS
-HI = lax.Precision.HIGHEST
 ROWS_T = (((1,), (1,)), ((), ()))
 COLS_T = (((0,), (0,)), ((), ()))
 PLAIN = (((1,), (0,)), ((), ()))
@@ -105,22 +104,19 @@
 
     def step(p, carry):
         here = pl.ds(pl.multiple_of(p * TILE, TILE), TILE)
-        tile = factor_tile(work[here, here])
-        upper = jnp.dot(tile, work[here, :], precision=HI, preferred_element_type=F32)
-        solved = jnp.dot(tile, x_ref[here, :], precision=HI, preferred_element_type=F32)
+        tile = split(factor_tile(work[here, here]))
+        upper = split(product(tile, split(work[here, :]), PLAIN))
+        solved = product(tile, split(x_ref[here, :]), PLAIN)
         x_ref[here, :] = solved
+        solved = split(solved)
         for q in range(first + 1, tiles):
 
             @pl.when(q > p)
             def _():
                 below = slice(q * TILE, (q + 1) * TILE)
-                part = upper[:, below]
-                work[below, :] -= lax.dot_general(
-                    part, upper, COLS_T, precision=HI, preferred_element_type=F32
-                )
-                x_ref[below, :] -= lax.dot_general(
-                    part, solved, COLS_T, precision=HI, preferred_element_type=F32
-                )
+                part = upper[0][:, below], upper[1][:, below]
+                work[below, :] -= product(part, upper, COLS_T)
+                x_ref[below, :] -= product(part, solved, COLS_T)
 
         return carry
 
@@ -162,15 +158,9 @@
 
 
 def weigh(rows_ref, primal_ref, dual_ref, by_primal, by_dual):
-    def part(i, carry):
-        half = primal_ref.shape[1] // 2
-        at = pl.ds(pl.multiple_of(i * half, half), half)
-        for source, target in ((primal_ref, by_primal), (dual_ref, by_dual)):
-            value = jnp.dot(rows_ref[...], source[:, at], preferred_element_type=F32)
-            target[:, at] = value.astype(BF16)
-        return carry
-
-    lax.fori_loop(0, 2, part, 0)
+    for source, target in ((primal_ref, by_primal), (dual_ref, by_dual)):
+        value = jnp.dot(rows_ref[...], source[...], preferred_element_type=F32)
+        target[...] = value.astype(BF16)
 
 
 def hadamard(by_primal, by_dual, columns):
@@ -427,8 +417,11 @@
     columns, primal_block, dual_block = vectors[0], primal[0], dual_inverse[0]
     order = [block_order(z, cones) for z in range(cones)]
 
-    def exchange(codes, pairs=lambda u: [(i, i ^ u) for i in range(cones)]):
-        return [lax.ppermute(code, "cone", pairs(u)) for u, code in enumerate(codes, 1)]
+    def exchange(codes):
+        return [
+            lax.ppermute(code, "cone", [(i, i ^ u) for i in range(cones)])
+            for u, code in enumerate(codes, 1)
+        ]
 
     def along(value, moves):
         pairs = [(a * owners + i, b * owners + i) for a, b in moves for i in range(owners)]
@@ -501,15 +494,7 @@
             half_own, half_code = codes[cones - 1 :]
         summed.append([first] + exchange(codes[: cones - 1]))
 
-    grid = ("cone", "con")
-    half_codes = [
-        lax.ppermute(
-            half_code,
-            grid,
-            [(c * con_count + i, (c ^ u) * con_count + i) for c in range(cones) for i in range(owners)],
-        )
-        for u in range(1, cones)
-    ]
+    half_codes = exchange([half_code] * (cones - 1))
     half = call(
         sum_half_kernel, shaped(coded_square, row_dev, I16), (half_own, *half_codes), limit=4
     )
@@ -565,7 +550,7 @@
         16,
         1,
     )
-    rest_codes = exchange(rest_codes, lambda u: [(i, i ^ u) for i in range(cones) if i ^ u])
+    rest_codes = exchange(rest_codes)
     factor_rows, row_factor = call(
         rows_kernel,
         (shaped(PANEL, per_block, F32), shaped(PANEL, PANEL, F32)),

time: 166 us -> 169 us (1.018)
  the two profiles are of different devices: /device:TPU:21 before, /device:TPU:22 now
where the time goes in v1:
time: 169 us; the launch traced here: 168 us
  waiting for transfers between devices  71.4 us (42%)
  Pallas kernels  51.9 us (31%)
  starting transfers between devices  43.9 us (26%)
    pallas_call x16, Pallas kernels, call(): pl.pallas_call(kernel, out_shape=out_shape, in_specs=[in_smem()] * scalar...  32.3 us
    ppermute x8, waiting for transfers between devices, along(): return lax.ppermute(value, 'con', pairs)  32.1 us
    ppermute x21, starting transfers between devices, exchange(): lax.ppermute(code, 'cone', [(i, i ^ u) for i in range(cones)])  29.5 us
    ppermute x21, waiting for transfers between devices, exchange(): lax.ppermute(code, 'cone', [(i, i ^ u) for i in range(cones)])  28 us
    pallas_call x2, Pallas kernels, eliminate(): pl.pallas_call(functools.partial(eliminate_kernel, first, last), out_shap...  18.3 us
    ppermute x3, waiting for transfers between devices, shards(): leads.append(lax.ppermute(lead, ('cone', 'con'), pairs))  11.3 us
    ppermute x8, starting transfers between devices, along(): return lax.ppermute(value, 'con', pairs)  11 us
  transfers between devices with their start and end apart: 38, of which 11 were waited for; matrix products, arithmetic and copies ran while one was open for 0% of the time, Pallas kernels for 28%

profile of v1, /device:TPU:22, one launch (start us, length us, event | category | flops | bytes accessed | tf_op | source)
XLA Modules:
  0.0 168.3 jit_solution(4429351599272188793)
XLA Ops:
  0.0 0.7 copy-done.3
  0.7 1.3 mask_rows.1.refs_0_
  1.9 1.6 collective-permute-start.11
  3.6 1.9 %collective-permute-start.17 = (bf16[256,1024]{1,0:T(8,128)(2,1)S(1)}, bf16[256,1024]{1,0:T(8,128)(2,1)S(1)}, u32[]{:S(2)}, u32[]{:S(2)}) collective-permute-start(bf16[256,1024]{1,0:T(8,128)(2,1)S(1)} %mask_rows.1.refs_0_), channel_id=1, source_target_pairs={{2,4},{3,5},{4,2},{5,3},{10,12},{11,13},{12,10},{13,11},{18,20},{1... | collective-permute-start | bytes 1572872 | tf_op jit(solution)/shard_map/ppermute | solution.py:428
  5.5 0.7 collective-permute-start.16
  6.2 10.6 %collective-permute-done.11.refs_0_ = bf16[256,1024]{1,0:T(8,128)(2,1)S(1)} collective-permute-done((bf16[256,1024]{1,0:T(8,128)(2,1)S(1)}, bf16[256,1024]{1,0:T(8,128)(2,1)S(1)}, u32[]{:S(2)}, u32[]{:S(2)}) %collective-permute-start.11) | collective-permute-done | bytes 524320 | tf_op jit(solution)/shard_map/ppermute | solution.py:428
  16.8 2.3 %collective-permute-start.18 = (bf16[256,1024]{1,0:T(8,128)(2,1)S(1)}, bf16[256,1024]{1,0:T(8,128)(2,1)S(1)}, u32[]{:S(2)}, u32[]{:S(2)}) collective-permute-start(bf16[256,1024]{1,0:T(8,128)(2,1)S(1)} %collective-permute-done.11.refs_0_), channel_id=1, source_target_pairs={{2,4},{3,5},{4,2},{5,3},{10,12},{11,13},{12,10},{13,11},{18,20},{1... | collective-permute-start | bytes 1572872 | tf_op jit(solution)/shard_map/ppermute | solution.py:428
  19.2 0.1 collective-permute-start
  19.2 0.1 shard_map.61.refs_0_
  19.3 0.5 collective-permute-start.12
  19.8 11.7 %collective-permute-done.17.refs_1_.refs_0_ = bf16[256,1024]{1,0:T(8,128)(2,1)S(1)} collective-permute-done((bf16[256,1024]{1,0:T(8,128)(2,1)S(1)}, bf16[256,1024]{1,0:T(8,128)(2,1)S(1)}, u32[]{:S(2)}, u32[]{:S(2)}) %collective-permute-start.17) | collective-permute-done | bytes 524320 | tf_op jit(solution)/shard_map/ppermute | solution.py:428
  31.5 9.8 %collective-permute-done.18.refs_2_ = bf16[256,1024]{1,0:T(8,128)(2,1)S(1)} collective-permute-done((bf16[256,1024]{1,0:T(8,128)(2,1)S(1)}, bf16[256,1024]{1,0:T(8,128)(2,1)S(1)}, u32[]{:S(2)}, u32[]{:S(2)}) %collective-permute-start.18) | collective-permute-done | bytes 524320 | tf_op jit(solution)/shard_map/ppermute | solution.py:428
  41.4 0.1 collective-permute-start.19
  41.5 5.7 %shard_map.55 = (f32[128,1024]{1,0:T(8,128)S(1)}, s16[136,1024]{1,0:T(8,128)(2,1)S(1)}, s16[136,1024]{1,0:T(8,128)(2,1)S(1)}, s16[136,1024]{1,0:T(8,128)(2,1)S(1...) custom-call(s32[1,8]{1,0:T(1,128)S(1)} %copy-done.4, bf16[256,1024]{1,0:T(8,128)(2,1)S(1)} %mask_rows.1.refs_0_, ...), custom_call_target="tpu_custom_call" | custom-call | tf_op jit(solution)/shard_map/pallas_call | solution.py:364
  47.2 0.6 collective-permute-start.8
  47.8 0.5 collective-permute-start.9
  48.3 1.5 collective-permute-start.30
  49.8 2.5 %collective-permute-start.10 = (s16[136,1024]{1,0:T(8,128)(2,1)S(1)}, s16[136,1024]{1,0:T(8,128)(2,1)S(1)}, u32[]{:S(2)}, u32[]{:S(2)}) collective-permute-start(s16[136,1024]{1,0:T(8,128)(2,1)S(1)} %get-tuple-element.48), channel_id=1, source_target_pairs={{0,24},{8,16},{16,8},{24,0},{1,25},{9,17},{17,9},{25,1},{2,26},{10... | collective-permute-start | bytes 835592 | tf_op jit(solution)/shard_map/ppermute | solution.py:422
  52.3 5.6 %shard_map.62 = (f32[128,1024]{1,0:T(8,128)S(1)}, s16[136,1024]{1,0:T(8,128)(2,1)S(1)}, s16[136,1024]{1,0:T(8,128)(2,1)S(1)}, s16[136,1024]{1,0:T(8,128)(2,1)S(1)}) custom-call(s32[1,8]{1,0:T(1,128)S(1)} %copy-done.4, bf16[256,1024]{1,0:T(8,128)(2,1)S(1)} %shard_map.61.refs_0_, bf16[256,1024]{1,0:T(8,128)(2,1)S(1)} %collective-permute-done.12.refs_1_, ...), custom_call_target="tpu_custom_call" | custom-call | tf_op jit(solution)/shard_map/pallas_call | solution.py:364
  57.9 0.6 collective-permute-start.13
  58.5 4.2 %collective-permute-done.9.refs_2_ = s16[136,1024]{1,0:T(8,128)(2,1)S(1)} collective-permute-done((s16[136,1024]{1,0:T(8,128)(2,1)S(1)}, s16[136,1024]{1,0:T(8,128)(2,1)S(1)}, u32[]{:S(2)}, u32[]{:S(2)}) %collective-permute-start.9) | collective-permute-done | bytes 278560 | tf_op jit(solution)/shard_map/ppermute | solution.py:422
  62.7 2.8 %collective-permute-start.15 = (s16[136,1024]{1,0:T(8,128)(2,1)S(1)}, s16[136,1024]{1,0:T(8,128)(2,1)S(1)}, u32[]{:S(2)}, u32[]{:S(2)}) collective-permute-start(s16[136,1024]{1,0:T(8,128)(2,1)S(1)} %get-tuple-element.52), channel_id=1, source_target_pairs={{0,24},{8,16},{16,8},{24,0},{1,25},{9,17},{17,9},{25,1},{2,26},{10... | collective-permute-start | bytes 835592 | tf_op jit(solution)/shard_map/ppermute | solution.py:422
  65.5 5.5 %shard_map.64 = (f32[128,1024]{1,0:T(8,128)S(1)}, s16[136,1024]{1,0:T(8,128)(2,1)S(1)}, s16[136,1024]{1,0:T(8,128)(2,1)S(1)}, s16[136,1024]{1,0:T(8,128)(2,1)S(1)}) custom-call(s32[1,8]{1,0:T(1,128)S(1)} %copy-done.4, bf16[256,1024]{1,0:T(8,128)(2,1)S(1)} %shard_map.63.refs_0_, bf16[256,1024]{1,0:T(8,128)(2,1)S(1)} %collective-permute-done.19.refs_1_, ...), custom_call_target="tpu_custom_call" | custom-call | tf_op jit(solution)/shard_map/pallas_call | solution.py:364
  71.0 0.8 collective-permute-start.20
  71.8 2.7 %collective-permute-start.22 = (s16[136,1024]{1,0:T(8,128)(2,1)S(1)}, s16[136,1024]{1,0:T(8,128)(2,1)S(1)}, u32[]{:S(2)}, u32[]{:S(2)}) collective-permute-start(s16[136,1024]{1,0:T(8,128)(2,1)S(1)} %get-tuple-element.56), channel_id=1, source_target_pairs={{0,24},{8,16},{16,8},{24,0},{1,25},{9,17},{17,9},{25,1},{2,26},{10... | collective-permute-start | bytes 835592 | tf_op jit(solution)/shard_map/ppermute | solution.py:422
  74.6 1.6 collective-permute-done.14.refs_6_
  76.2 3.0 %collective-permute-start.3 = (s16[544,256]{1,0:T(8,128)(2,1)S(1)}, s16[544,256]{1,0:T(8,128)(2,1)S(1)}, u32[]{:S(2)}, u32[]{:S(2)}) collective-permute-start(s16[544,256]{1,0:T(8,128)(2,1)S(1)} %get-tuple-element.39), channel_id=1, source_target_pairs={{0,24},{8,16},{16,8},{24,0},{1,25},{9,17},{17,9},{25,1},{2,26},{10... | collective-permute-start | bytes 835592 | tf_op jit(solution)/shard_map/ppermute | solution.py:422
  79.2 0.1 collective-permute-start.31
  79.3 1.4 collective-permute-done.20.refs_9_
  80.7 0.5 collective-permute-start.2
  81.2 12.8 %collective-permute-done.21.refs_10_ = s16[136,1024]{1,0:T(8,128)(2,1)S(1)} collective-permute-done((s16[136,1024]{1,0:T(8,128)(2,1)S(1)}, s16[136,1024]{1,0:T(8,128)(2,1)S(1)}, u32[]{:S(2)}, u32[]{:S(2)}) %collective-permute-start.21) | collective-permute-done | bytes 278560 | tf_op jit(solution)/shard_map/ppermute | solution.py:422
  94.0 3.4 %collective-permute-start.1 = (s16[544,256]{1,0:T(8,128)(2,1)S(1)}, s16[544,256]{1,0:T(8,128)(2,1)S(1)}, u32[]{:S(2)}, u32[]{:S(2)}) collective-permute-start(s16[544,256]{1,0:T(8,128)(2,1)S(1)} %get-tuple-element.39), channel_id=1, source_target_pairs={{0,8},{8,0},{16,24},{24,16},{1,9},{9,1},{17,25},{25,17},{2,10},{10... | collective-permute-start | bytes 835592 | tf_op jit(solution)/shard_map/ppermute | solution.py:422
  97.4 0.4 shard_map.65
  97.8 0.1 collective-permute-start.25
  97.9 1.4 collective-permute-start.24
  99.3 3.6 %collective-permute-done.2.refs_1_ = s16[544,256]{1,0:T(8,128)(2,1)S(1)} collective-permute-done((s16[544,256]{1,0:T(8,128)(2,1)S(1)}, s16[544,256]{1,0:T(8,128)(2,1)S(1)}, u32[]{:S(2)}, u32[]{:S(2)}) %collective-permute-start.2) | collective-permute-done | bytes 278560 | tf_op jit(solution)/shard_map/ppermute | solution.py:422
  102.9 3.4 %collective-permute-start.23 = (s16[136,1024]{1,0:T(8,128)(2,1)S(1)}, s16[136,1024]{1,0:T(8,128)(2,1)S(1)}, u32[]{:S(2)}, u32[]{:S(2)}) collective-permute-start(s16[136,1024]{1,0:T(8,128)(2,1)S(1)} %get-tuple-element.58), channel_id=1, source_target_pairs={{0,8},{8,0},{16,24},{24,16},{1,9},{9,1},{17,25},{25,17},{2,10},{10... | collective-permute-start | bytes 835592 | tf_op jit(solution)/shard_map/ppermute | solution.py:422
  106.4 0.4 shard_map.56.refs_0_
  106.7 0.7 collective-permute-start.6
  107.4 1.5 collective-permute-start.5
  108.9 5.6 %shard_map.70 = (f32[128,1024]{1,0:T(8,128)S(1)}, s16[136,1024]{1,0:T(8,128)(2,1)S(1)}, s16[136,1024]{1,0:T(8,128)(2,1)S(1)}, s16[136,1024]{1,0:T(8,128)(2,1)S(1)}) custom-call(s32[1,8]{1,0:T(1,128)S(1)} %copy-done.4, bf16[256,1024]{1,0:T(8,128)(2,1)S(1)} %shard_map.69.refs_0_, bf16[256,1024]{1,0:T(8,128)(2,1)S(1)} %collective-permute-done.31.refs_1_, ...), custom_call_target="tpu_custom_call" | custom-call | tf_op jit(solution)/shard_map/pallas_call | solution.py:364
  114.5 0.0 copy-start.5
  114.5 0.7 collective-permute-start.4
  115.2 0.6 collective-permute-start.32
  115.8 0.2 collective-permute-start.33
  116.1 0.4 shard_map.66
  116.5 2.8 %collective-permute-start.34 = (s16[136,1024]{1,0:T(8,128)(2,1)S(1)}, s16[136,1024]{1,0:T(8,128)(2,1)S(1)}, u32[]{:S(2)}, u32[]{:S(2)}) collective-permute-start(s16[136,1024]{1,0:T(8,128)(2,1)S(1)} %get-tuple-element.66), channel_id=1, source_target_pairs={{0,24},{8,16},{16,8},{24,0},{1,25},{9,17},{17,9},{25,1},{2,26},{10... | collective-permute-start | bytes 835592 | tf_op jit(solution)/shard_map/ppermute | solution.py:422
  119.3 0.7 collective-permute-start.28
  120.0 0.7 collective-permute-start.27
  120.7 1.4 collective-permute-done.32.refs_13_
  122.1 1.3 collective-permute-start.26
  123.4 2.9 %collective-permute-done.33.refs_14_ = s16[136,1024]{1,0:T(8,128)(2,1)S(1)} collective-permute-done((s16[136,1024]{1,0:T(8,128)(2,1)S(1)}, s16[136,1024]{1,0:T(8,128)(2,1)S(1)}, u32[]{:S(2)}, u32[]{:S(2)}) %collective-permute-start.33) | collective-permute-done | bytes 278560 | tf_op jit(solution)/shard_map/ppermute | solution.py:422
  126.3 1.6 shard_map.71
  128.0 11.3 %collective-permute-done.26.refs_1_ = s16[544,256]{1,0:T(8,128)(2,1)S(1)} collective-permute-done((s16[544,256]{1,0:T(8,128)(2,1)S(1)}, s16[544,256]{1,0:T(8,128)(2,1)S(1)}, u32[]{:S(2)}, u32[]{:S(2)}) %collective-permute-start.26) | collective-permute-done | bytes 278560 | tf_op jit(solution)/shard_map/ppermute | solution.py:538
  139.2 0.3 shard_map.67.refs_0_
  139.5 0.1 collective-permute-start.29
  139.6 0.1 collective-permute-start.35
  139.7 0.1 collective-permute-start.36
  139.8 3.4 %collective-permute-start.37 = (s16[136,1024]{1,0:T(8,128)(2,1)S(1)}, s16[136,1024]{1,0:T(8,128)(2,1)S(1)}, u32[]{:S(2)}, u32[]{:S(2)}) collective-permute-start(s16[136,1024]{1,0:T(8,128)(2,1)S(1)} %get-tuple-element.70), channel_id=1, source_target_pairs={{0,24},{8,16},{16,8},{24,0},{1,25},{9,17},{17,9},{25,1},{2,26},{10... | collective-permute-start | bytes 835592 | tf_op jit(solution)/shard_map/ppermute | solution.py:422
  143.2 0.7 shard_map.58
  143.8 9.9 %shard_map.59 = (f32[512,512]{1,0:T(8,128)S(1)}, f32[512,512]{1,0:T(8,128)S(1)}) custom-call(f32[512,512]{1,0:T(8,128)S(1)} %get-tuple-element.40.work_in, f32[512,512]{1,0:T(8,128)S(1)} %get-tuple-element.41.x_in), custom_call_target="tpu_custom_call", output_to_operand_aliasing={{0}: (0, {}), {1}: (1, {})} | custom-call | tf_op jit(solution)/shard_map/pallas_call | solution.py:128
  153.8 8.4 %shard_map.60 = (f32[512,512]{1,0:T(8,128)S(1)}, f32[512,512]{1,0:T(8,128)S(1)}) custom-call(f32[512,512]{1,0:T(8,128)S(1)} %get-tuple-element.42.work_in, f32[512,512]{1,0:T(8,128)S(1)} %get-tuple-element.43.x_in), custom_call_target="tpu_custom_call", output_to_operand_aliasing={{0}: (0, {}), {1}: (1, {})} | custom-call | tf_op jit(solution)/shard_map/pallas_call | solution.py:128
  162.2 2.7 %shard_map.68 = (f32[512,1024]{1,0:T(8,128)S(1)}, f32[512,512]{1,0:T(8,128)S(1)}) custom-call(f32[512,512]{1,0:T(8,128)S(1)} %get-tuple-element.44.inverse_ref, f32[512,1024]{1,0:T(8,128)S(1)} %get-tuple-element.59.panel_ref, s16[544,256]{1,0:T(8,128)(2,1)S(1)} %shard_map.67.refs_0_, s16[544,256]{1,0:T(8,128)(2,1)S(1)} %collective-permute-done.29.refs_1_), custom_call_target="tpu_custom_call" | custom-call | tf_op jit(solution)/shard_map/pallas_call | solution.py:364
  164.9 3.3 %shard_map.72 = f32[512,1024]{1,0:T(8,128)} custom-call(f32[512,1024]{1,0:T(8,128)S(1)} %get-tuple-element.61.factor_ref, f32[512,512]{1,0:T(8,128)S(1)} %get-tuple-element.62.row_ref, f32[128,1024]{1,0:T(8,128)S(1)} %get-tuple-element.67.own_ref, s16[136,1024]{1,0:T(8,128)(2,1)S(1)} %collective-permute-done.35.refs_0_, ...), custom_call_target="tpu_custom_call" | custom-call | tf_op jit(solution)/shard_map/pallas_call | solution.py:364
  (43 shorter events, 0.2 us)
Async XLA Ops:
  0.0 0.7 copy-start.3
  0.7 40.8 %copy-start.1 = (bf16[1,1024,1024]{2,1,0:T(8,128)(2,1)S(1)}, bf16[1,1024,1024]{2,1,0:T(8,128)(2,1)}, u32[]{:S(2)}) copy-start(bf16[1,1024,1024]{2,1,0:T(8,128)(2,1)} %param.6) | copy-start | bytes 6291460
  0.7 40.8 %copy-start.2 = (bf16[1,1024,1024]{2,1,0:T(8,128)(2,1)S(1)}, bf16[1,1024,1024]{2,1,0:T(8,128)(2,1)}, u32[]{:S(2)}) copy-start(bf16[1,1024,1024]{2,1,0:T(8,128)(2,1)} %param.7) | copy-start | bytes 6291460
  1.9 39.6 %copy-start = (bf16[1,1024,1024]{2,1,0:T(8,128)(2,1)S(1)}, bf16[1,1024,1024]{2,1,0:T(8,128)(2,1)}, u32[]{:S(2)}) copy-start(bf16[1,1024,1024]{2,1,0:T(8,128)(2,1)} %param.5) | copy-start | bytes 6291460
  1.9 39.6 %copy-start.4 = (s32[1,8]{1,0:T(1,128)S(1)}, s32[1,8]{1,0:T(1,128)}, u32[]{:S(2)}) copy-start(s32[1,8]{1,0:T(1,128)} %touches_ref.9) | copy-start | bytes 100
  1.9 14.9 %collective-permute-start.11 = (bf16[256,1024]{1,0:T(8,128)(2,1)S(1)}, bf16[256,1024]{1,0:T(8,128)(2,1)S(1)}, u32[]{:S(2)}, u32[]{:S(2)}) collective-permute-start(bf16[256,1024]{1,0:T(8,128)(2,1)S(1)} %mask_rows.1.refs_0_), channel_id=1, source_target_pairs={{0,2},{1,3},{2,0},{3,1},{4,6},{5,7},{6,4},{7,5},{8,10},{9,11},{10,... | collective-permute-start | bytes 1572872 | tf_op jit(solution)/shard_map/ppermute | solution.py:428
  3.6 27.9 %collective-permute-start.17 = (bf16[256,1024]{1,0:T(8,128)(2,1)S(1)}, bf16[256,1024]{1,0:T(8,128)(2,1)S(1)}, u32[]{:S(2)}, u32[]{:S(2)}) collective-permute-start(bf16[256,1024]{1,0:T(8,128)(2,1)S(1)} %mask_rows.1.refs_0_), channel_id=1, source_target_pairs={{2,4},{3,5},{4,2},{5,3},{10,12},{11,13},{12,10},{13,11},{18,20},{1... | collective-permute-start | bytes 1572872 | tf_op jit(solution)/shard_map/ppermute | solution.py:428
  5.5 26.0 %collective-permute-start.16 = (bf16[256,1024]{1,0:T(8,128)(2,1)S(1)}, bf16[256,1024]{1,0:T(8,128)(2,1)S(1)}, u32[]{:S(2)}, u32[]{:S(2)}) collective-permute-start(bf16[256,1024]{1,0:T(8,128)(2,1)S(1)} %mask_rows.1.refs_0_), channel_id=1, source_target_pairs={{0,6},{1,7},{6,0},{7,1},{8,14},{9,15},{14,8},{15,9},{16,22},{17,23... | collective-permute-start | bytes 1572872 | tf_op jit(solution)/shard_map/ppermute | solution.py:428
  16.8 24.5 %collective-permute-start.18 = (bf16[256,1024]{1,0:T(8,128)(2,1)S(1)}, bf16[256,1024]{1,0:T(8,128)(2,1)S(1)}, u32[]{:S(2)}, u32[]{:S(2)}) collective-permute-start(bf16[256,1024]{1,0:T(8,128)(2,1)S(1)} %collective-permute-done.11.refs_0_), channel_id=1, source_target_pairs={{2,4},{3,5},{4,2},{5,3},{10,12},{11,13},{12,10},{13,11},{18,20},{1... | collective-permute-start | bytes 1572872 | tf_op jit(solution)/shard_map/ppermute | solution.py:428
  19.2 22.3 %collective-permute-start = (bf16[256,1024]{1,0:T(8,128)(2,1)S(1)}, bf16[256,1024]{1,0:T(8,128)(2,1)S(1)}, u32[]{:S(2)}, u32[]{:S(2)}) collective-permute-start(bf16[256,1024]{1,0:T(8,128)(2,1)S(1)} %mask_rows.1.refs_0_), channel_id=1, source_target_pairs={{0,1},{1,0},{2,3},{3,2},{4,5},{5,4},{6,7},{7,6},{8,9},{9,8},{10,11... | collective-permute-start | bytes 1572872 | tf_op jit(solution)/shard_map/ppermute | solution.py:438
  19.3 30.5 %collective-permute-start.12 = (bf16[256,1024]{1,0:T(8,128)(2,1)S(1)}, bf16[256,1024]{1,0:T(8,128)(2,1)S(1)}, u32[]{:S(2)}, u32[]{:S(2)}) collective-permute-start(bf16[256,1024]{1,0:T(8,128)(2,1)S(1)} %shard_map.61.refs_0_), channel_id=1, source_target_pairs={{0,1},{1,0},{2,3},{3,2},{4,5},{5,4},{6,7},{7,6},{8,9},{9,8},{10,11... | collective-permute-start | bytes 1572872 | tf_op jit(solution)/shard_map/ppermute | solution.py:438
  41.4 21.3 %collective-permute-start.19 = (bf16[256,1024]{1,0:T(8,128)(2,1)S(1)}, bf16[256,1024]{1,0:T(8,128)(2,1)S(1)}, u32[]{:S(2)}, u32[]{:S(2)}) collective-permute-start(bf16[256,1024]{1,0:T(8,128)(2,1)S(1)} %shard_map.63.refs_0_), channel_id=1, source_target_pairs={{0,1},{1,0},{2,3},{3,2},{4,5},{5,4},{6,7},{7,6},{8,9},{9,8},{10,11... | collective-permute-start | bytes 1572872 | tf_op jit(solution)/shard_map/ppermute | solution.py:438
  47.2 10.7 %collective-permute-start.8 = (s16[136,1024]{1,0:T(8,128)(2,1)S(1)}, s16[136,1024]{1,0:T(8,128)(2,1)S(1)}, u32[]{:S(2)}, u32[]{:S(2)}) collective-permute-start(s16[136,1024]{1,0:T(8,128)(2,1)S(1)} %get-tuple-element.46), channel_id=1, source_target_pairs={{0,8},{8,0},{16,24},{24,16},{1,9},{9,1},{17,25},{25,17},{2,10},{10... | collective-permute-start | bytes 835592 | tf_op jit(solution)/shard_map/ppermute | solution.py:422
  47.8 14.9 %collective-permute-start.9 = (s16[136,1024]{1,0:T(8,128)(2,1)S(1)}, s16[136,1024]{1,0:T(8,128)(2,1)S(1)}, u32[]{:S(2)}, u32[]{:S(2)}) collective-permute-start(s16[136,1024]{1,0:T(8,128)(2,1)S(1)} %get-tuple-element.47), channel_id=1, source_target_pairs={{0,16},{8,24},{16,0},{24,8},{1,17},{9,25},{17,1},{25,9},{2,18},{10... | collective-permute-start | bytes 835592 | tf_op jit(solution)/shard_map/ppermute | solution.py:422
  48.3 23.6 %collective-permute-start.30 = (bf16[256,1024]{1,0:T(8,128)(2,1)S(1)}, bf16[256,1024]{1,0:T(8,128)(2,1)S(1)}, u32[]{:S(2)}, u32[]{:S(2)}) collective-permute-start(bf16[256,1024]{1,0:T(8,128)(2,1)S(1)} %collective-permute-done.17.refs_1_.refs_0_), channel_id=1, source_target_pairs={{2,0},{3,1},{4,6},{5,7},{10,8},{11,9},{12,14},{13,15},{18,16},{19,... | collective-permute-start | bytes 1572872 | tf_op jit(solution)/shard_map/ppermute | solution.py:428
  49.8 21.2 %collective-permute-start.10 = (s16[136,1024]{1,0:T(8,128)(2,1)S(1)}, s16[136,1024]{1,0:T(8,128)(2,1)S(1)}, u32[]{:S(2)}, u32[]{:S(2)}) collective-permute-start(s16[136,1024]{1,0:T(8,128)(2,1)S(1)} %get-tuple-element.48), channel_id=1, source_target_pairs={{0,24},{8,16},{16,8},{24,0},{1,25},{9,17},{17,9},{25,1},{2,26},{10... | collective-permute-start | bytes 835592 | tf_op jit(solution)/shard_map/ppermute | solution.py:422
  57.9 14.0 %collective-permute-start.13 = (s16[136,1024]{1,0:T(8,128)(2,1)S(1)}, s16[136,1024]{1,0:T(8,128)(2,1)S(1)}, u32[]{:S(2)}, u32[]{:S(2)}) collective-permute-start(s16[136,1024]{1,0:T(8,128)(2,1)S(1)} %get-tuple-element.50), channel_id=1, source_target_pairs={{0,8},{8,0},{16,24},{24,16},{1,9},{9,1},{17,25},{25,17},{2,10},{10... | collective-permute-start | bytes 835592 | tf_op jit(solution)/shard_map/ppermute | solution.py:422
  62.7 13.5 %collective-permute-start.14 = (s16[136,1024]{1,0:T(8,128)(2,1)S(1)}, s16[136,1024]{1,0:T(8,128)(2,1)S(1)}, u32[]{:S(2)}, u32[]{:S(2)}) collective-permute-start(s16[136,1024]{1,0:T(8,128)(2,1)S(1)} %get-tuple-element.51), channel_id=1, source_target_pairs={{0,16},{8,24},{16,0},{24,8},{1,17},{9,25},{17,1},{25,9},{2,18},{10... | collective-permute-start | bytes 835592 | tf_op jit(solution)/shard_map/ppermute | solution.py:422
  62.7 16.5 %collective-permute-start.15 = (s16[136,1024]{1,0:T(8,128)(2,1)S(1)}, s16[136,1024]{1,0:T(8,128)(2,1)S(1)}, u32[]{:S(2)}, u32[]{:S(2)}) collective-permute-start(s16[136,1024]{1,0:T(8,128)(2,1)S(1)} %get-tuple-element.52), channel_id=1, source_target_pairs={{0,24},{8,16},{16,8},{24,0},{1,25},{9,17},{17,9},{25,1},{2,26},{10... | collective-permute-start | bytes 835592 | tf_op jit(solution)/shard_map/ppermute | solution.py:422
  71.0 9.7 %collective-permute-start.20 = (s16[136,1024]{1,0:T(8,128)(2,1)S(1)}, s16[136,1024]{1,0:T(8,128)(2,1)S(1)}, u32[]{:S(2)}, u32[]{:S(2)}) collective-permute-start(s16[136,1024]{1,0:T(8,128)(2,1)S(1)} %get-tuple-element.54), channel_id=1, source_target_pairs={{0,8},{8,0},{16,24},{24,16},{1,9},{9,1},{17,25},{25,17},{2,10},{10... | collective-permute-start | bytes 835592 | tf_op jit(solution)/shard_map/ppermute | solution.py:422
  71.8 22.2 %collective-permute-start.21 = (s16[136,1024]{1,0:T(8,128)(2,1)S(1)}, s16[136,1024]{1,0:T(8,128)(2,1)S(1)}, u32[]{:S(2)}, u32[]{:S(2)}) collective-permute-start(s16[136,1024]{1,0:T(8,128)(2,1)S(1)} %get-tuple-element.55), channel_id=1, source_target_pairs={{0,16},{8,24},{16,0},{24,8},{1,17},{9,25},{17,1},{25,9},{2,18},{10... | collective-permute-start | bytes 835592 | tf_op jit(solution)/shard_map/ppermute | solution.py:422
  71.8 25.6 %collective-permute-start.22 = (s16[136,1024]{1,0:T(8,128)(2,1)S(1)}, s16[136,1024]{1,0:T(8,128)(2,1)S(1)}, u32[]{:S(2)}, u32[]{:S(2)}) collective-permute-start(s16[136,1024]{1,0:T(8,128)(2,1)S(1)} %get-tuple-element.56), channel_id=1, source_target_pairs={{0,24},{8,16},{16,8},{24,0},{1,25},{9,17},{17,9},{25,1},{2,26},{10... | collective-permute-start | bytes 835592 | tf_op jit(solution)/shard_map/ppermute | solution.py:422
  76.2 21.7 %collective-permute-start.3 = (s16[544,256]{1,0:T(8,128)(2,1)S(1)}, s16[544,256]{1,0:T(8,128)(2,1)S(1)}, u32[]{:S(2)}, u32[]{:S(2)}) collective-permute-start(s16[544,256]{1,0:T(8,128)(2,1)S(1)} %get-tuple-element.39), channel_id=1, source_target_pairs={{0,24},{8,16},{16,8},{24,0},{1,25},{9,17},{17,9},{25,1},{2,26},{10... | collective-permute-start | bytes 835592 | tf_op jit(solution)/shard_map/ppermute | solution.py:422
  79.2 28.2 %collective-permute-start.31 = (bf16[256,1024]{1,0:T(8,128)(2,1)S(1)}, bf16[256,1024]{1,0:T(8,128)(2,1)S(1)}, u32[]{:S(2)}, u32[]{:S(2)}) collective-permute-start(bf16[256,1024]{1,0:T(8,128)(2,1)S(1)} %shard_map.69.refs_0_), channel_id=1, source_target_pairs={{0,1},{1,0},{2,3},{3,2},{4,5},{5,4},{6,7},{7,6},{8,9},{9,8},{10,11... | collective-permute-start | bytes 1572872 | tf_op jit(solution)/shard_map/ppermute | solution.py:438
  80.7 22.2 %collective-permute-start.2 = (s16[544,256]{1,0:T(8,128)(2,1)S(1)}, s16[544,256]{1,0:T(8,128)(2,1)S(1)}, u32[]{:S(2)}, u32[]{:S(2)}) collective-permute-start(s16[544,256]{1,0:T(8,128)(2,1)S(1)} %get-tuple-element.39), channel_id=1, source_target_pairs={{0,16},{8,24},{16,0},{24,8},{1,17},{9,25},{17,1},{25,9},{2,18},{10... | collective-permute-start | bytes 835592 | tf_op jit(solution)/shard_map/ppermute | solution.py:422
  94.0 12.3 %collective-permute-start.1 = (s16[544,256]{1,0:T(8,128)(2,1)S(1)}, s16[544,256]{1,0:T(8,128)(2,1)S(1)}, u32[]{:S(2)}, u32[]{:S(2)}) collective-permute-start(s16[544,256]{1,0:T(8,128)(2,1)S(1)} %get-tuple-element.39), channel_id=1, source_target_pairs={{0,8},{8,0},{16,24},{24,16},{1,9},{9,1},{17,25},{25,17},{2,10},{10... | collective-permute-start | bytes 835592 | tf_op jit(solution)/shard_map/ppermute | solution.py:422
  97.8 16.7 %collective-permute-start.25 = (s16[136,1024]{1,0:T(8,128)(2,1)S(1)}, s16[136,1024]{1,0:T(8,128)(2,1)S(1)}, u32[]{:S(2)}, u32[]{:S(2)}) collective-permute-start(s16[136,1024]{1,0:T(8,128)(2,1)S(1)} %get-tuple-element.58), channel_id=1, source_target_pairs={{0,24},{8,16},{16,8},{24,0},{1,25},{9,17},{17,9},{25,1},{2,26},{10... | collective-permute-start | bytes 835592 | tf_op jit(solution)/shard_map/ppermute | solution.py:422
  97.9 17.3 %collective-permute-start.24 = (s16[136,1024]{1,0:T(8,128)(2,1)S(1)}, s16[136,1024]{1,0:T(8,128)(2,1)S(1)}, u32[]{:S(2)}, u32[]{:S(2)}) collective-permute-start(s16[136,1024]{1,0:T(8,128)(2,1)S(1)} %get-tuple-element.58), channel_id=1, source_target_pairs={{0,16},{8,24},{16,0},{24,8},{1,17},{9,25},{17,1},{25,9},{2,18},{10... | collective-permute-start | bytes 835592 | tf_op jit(solution)/shard_map/ppermute | solution.py:422
  102.9 12.9 %collective-permute-start.23 = (s16[136,1024]{1,0:T(8,128)(2,1)S(1)}, s16[136,1024]{1,0:T(8,128)(2,1)S(1)}, u32[]{:S(2)}, u32[]{:S(2)}) collective-permute-start(s16[136,1024]{1,0:T(8,128)(2,1)S(1)} %get-tuple-element.58), channel_id=1, source_target_pairs={{0,8},{8,0},{16,24},{24,16},{1,9},{9,1},{17,25},{25,17},{2,10},{10... | collective-permute-start | bytes 835592 | tf_op jit(solution)/shard_map/ppermute | solution.py:422
  106.7 9.8 %collective-permute-start.6 = (s16[544,256]{1,0:T(8,128)(2,1)S(1)}, s16[544,256]{1,0:T(8,128)(2,1)S(1)}, u32[]{:S(2)}, u32[]{:S(2)}) collective-permute-start(s16[544,256]{1,0:T(8,128)(2,1)S(1)} %shard_map.56.refs_0_), channel_id=1, source_target_pairs={{0,6},{1,7},{8,14},{9,15},{16,22},{17,23},{24,30},{25,31}} | collective-permute-start | bytes 835592 | tf_op jit(solution)/shard_map/ppermute | solution.py:428
  107.4 11.9 %collective-permute-start.5 = (s16[544,256]{1,0:T(8,128)(2,1)S(1)}, s16[544,256]{1,0:T(8,128)(2,1)S(1)}, u32[]{:S(2)}, u32[]{:S(2)}) collective-permute-start(s16[544,256]{1,0:T(8,128)(2,1)S(1)} %shard_map.56.refs_0_), channel_id=1, source_target_pairs={{0,4},{1,5},{8,12},{9,13},{16,20},{17,21},{24,28},{25,29}} | collective-permute-start | bytes 835592 | tf_op jit(solution)/shard_map/ppermute | solution.py:428
  114.5 11.8 %copy-start.5 = (s32[4,4]{1,0:T(4,128)S(1)}, s32[4,4]{1,0:T(4,128)}, u32[]{:S(2)}) copy-start(s32[4,4]{1,0:T(4,128)} %constant.2.clone.order_ref) | copy-start | bytes 196
  114.5 5.4 %collective-permute-start.4 = (s16[544,256]{1,0:T(8,128)(2,1)S(1)}, s16[544,256]{1,0:T(8,128)(2,1)S(1)}, u32[]{:S(2)}, u32[]{:S(2)}) collective-permute-start(s16[544,256]{1,0:T(8,128)(2,1)S(1)} %shard_map.56.refs_0_), channel_id=1, source_target_pairs={{0,2},{1,3},{8,10},{9,11},{16,18},{17,19},{24,26},{25,27}} | collective-permute-start | bytes 835592 | tf_op jit(solution)/shard_map/ppermute | solution.py:428
  115.2 6.9 %collective-permute-start.32 = (s16[136,1024]{1,0:T(8,128)(2,1)S(1)}, s16[136,1024]{1,0:T(8,128)(2,1)S(1)}, u32[]{:S(2)}, u32[]{:S(2)}) collective-permute-start(s16[136,1024]{1,0:T(8,128)(2,1)S(1)} %get-tuple-element.64), channel_id=1, source_target_pairs={{0,8},{8,0},{16,24},{24,16},{1,9},{9,1},{17,25},{25,17},{2,10},{10... | collective-permute-start | bytes 835592 | tf_op jit(solution)/shard_map/ppermute | solution.py:422
  115.8 10.5 %collective-permute-start.33 = (s16[136,1024]{1,0:T(8,128)(2,1)S(1)}, s16[136,1024]{1,0:T(8,128)(2,1)S(1)}, u32[]{:S(2)}, u32[]{:S(2)}) collective-permute-start(s16[136,1024]{1,0:T(8,128)(2,1)S(1)} %get-tuple-element.65), channel_id=1, source_target_pairs={{0,16},{8,24},{16,0},{24,8},{1,17},{9,25},{17,1},{25,9},{2,18},{10... | collective-permute-start | bytes 835592 | tf_op jit(solution)/shard_map/ppermute | solution.py:422
  116.5 9.8 %collective-permute-start.34 = (s16[136,1024]{1,0:T(8,128)(2,1)S(1)}, s16[136,1024]{1,0:T(8,128)(2,1)S(1)}, u32[]{:S(2)}, u32[]{:S(2)}) collective-permute-start(s16[136,1024]{1,0:T(8,128)(2,1)S(1)} %get-tuple-element.66), channel_id=1, source_target_pairs={{0,24},{8,16},{16,8},{24,0},{1,25},{9,17},{17,9},{25,1},{2,26},{10... | collective-permute-start | bytes 835592 | tf_op jit(solution)/shard_map/ppermute | solution.py:422
  119.3 8.7 %collective-permute-start.28 = (s16[544,256]{1,0:T(8,128)(2,1)S(1)}, s16[544,256]{1,0:T(8,128)(2,1)S(1)}, u32[]{:S(2)}, u32[]{:S(2)}) collective-permute-start(s16[544,256]{1,0:T(8,128)(2,1)S(1)} %get-tuple-element.60.refs_0_), channel_id=1, source_target_pairs={{10,12},{11,13},{20,18},{21,19},{30,24},{31,25}} | collective-permute-start | bytes 835592 | tf_op jit(solution)/shard_map/ppermute | solution.py:538
  120.0 8.0 %collective-permute-start.27 = (s16[544,256]{1,0:T(8,128)(2,1)S(1)}, s16[544,256]{1,0:T(8,128)(2,1)S(1)}, u32[]{:S(2)}, u32[]{:S(2)}) collective-permute-start(s16[544,256]{1,0:T(8,128)(2,1)S(1)} %get-tuple-element.60.refs_0_), channel_id=1, source_target_pairs={{10,14},{11,15},{20,16},{21,17},{30,26},{31,27}} | collective-permute-start | bytes 835592 | tf_op jit(solution)/shard_map/ppermute | solution.py:538
  122.1 17.1 %collective-permute-start.26 = (s16[544,256]{1,0:T(8,128)(2,1)S(1)}, s16[544,256]{1,0:T(8,128)(2,1)S(1)}, u32[]{:S(2)}, u32[]{:S(2)}) collective-permute-start(s16[544,256]{1,0:T(8,128)(2,1)S(1)} %get-tuple-element.60.refs_0_), channel_id=1, source_target_pairs={{10,8},{11,9},{20,22},{21,23},{30,28},{31,29}} | collective-permute-start | bytes 835592 | tf_op jit(solution)/shard_map/ppermute | solution.py:538
  126.3 16.8 %collective-permute-start.7 = (s16[544,256]{1,0:T(8,128)(2,1)S(1)}, s16[544,256]{1,0:T(8,128)(2,1)S(1)}, u32[]{:S(2)}, u32[]{:S(2)}) collective-permute-start(s16[544,256]{1,0:T(8,128)(2,1)S(1)} %shard_map.57.refs_0_), channel_id=1, source_target_pairs={{0,1},{1,0},{2,3},{3,2},{4,5},{5,4},{6,7},{7,6},{8,9},{9,8},{10,11... | collective-permute-start | bytes 835592 | tf_op jit(solution)/shard_map/ppermute | solution.py:438
  139.5 22.7 %collective-permute-start.29 = (s16[544,256]{1,0:T(8,128)(2,1)S(1)}, s16[544,256]{1,0:T(8,128)(2,1)S(1)}, u32[]{:S(2)}, u32[]{:S(2)}) collective-permute-start(s16[544,256]{1,0:T(8,128)(2,1)S(1)} %shard_map.67.refs_0_), channel_id=1, source_target_pairs={{0,1},{1,0},{2,3},{3,2},{4,5},{5,4},{6,7},{7,6},{8,9},{9,8},{10,11... | collective-permute-start | bytes 835592 | tf_op jit(solution)/shard_map/ppermute | solution.py:438
  139.6 25.3 %collective-permute-start.35 = (s16[136,1024]{1,0:T(8,128)(2,1)S(1)}, s16[136,1024]{1,0:T(8,128)(2,1)S(1)}, u32[]{:S(2)}, u32[]{:S(2)}) collective-permute-start(s16[136,1024]{1,0:T(8,128)(2,1)S(1)} %get-tuple-element.68), channel_id=1, source_target_pairs={{0,8},{8,0},{16,24},{24,16},{1,9},{9,1},{17,25},{25,17},{2,10},{10... | collective-permute-start | bytes 835592 | tf_op jit(solution)/shard_map/ppermute | solution.py:422
  139.7 25.2 %collective-permute-start.36 = (s16[136,1024]{1,0:T(8,128)(2,1)S(1)}, s16[136,1024]{1,0:T(8,128)(2,1)S(1)}, u32[]{:S(2)}, u32[]{:S(2)}) collective-permute-start(s16[136,1024]{1,0:T(8,128)(2,1)S(1)} %get-tuple-element.69), channel_id=1, source_target_pairs={{0,16},{8,24},{16,0},{24,8},{1,17},{9,25},{17,1},{25,9},{2,18},{10... | collective-permute-start | bytes 835592 | tf_op jit(solution)/shard_map/ppermute | solution.py:422
  139.8 25.2 %collective-permute-start.37 = (s16[136,1024]{1,0:T(8,128)(2,1)S(1)}, s16[136,1024]{1,0:T(8,128)(2,1)S(1)}, u32[]{:S(2)}, u32[]{:S(2)}) collective-permute-start(s16[136,1024]{1,0:T(8,128)(2,1)S(1)} %get-tuple-element.70), channel_id=1, source_target_pairs={{0,24},{8,16},{16,8},{24,0},{1,25},{9,17},{17,9},{25,1},{2,26},{10... | collective-permute-start | bytes 835592 | tf_op jit(solution)/shard_map/ppermute | solution.py:422

commit v2 on v1

--- a/solution.py
+++ b/solution.py
@@ -325,18 +325,20 @@
             out_ref[...] = in_ref[...]
 
 
-def rows_kernel(inverse_ref, panel_ref, *refs):
-    *lead_refs, factor_ref, row_ref, lead = refs
+def factor_rows_kernel(inverse_ref, panel_ref, factor_ref):
+    factor_ref[...] = product(split(inverse_ref[...]), split(panel_ref[...]), PLAIN)
+
+
+def rows_kernel(inverse_ref, *refs):
+    *lead_refs, row_ref, lead = refs
     owners = len(lead_refs)
     width = lead_refs[0].shape[1]
     core = lax.rem(lax.axis_index("con"), owners)
     for s, lead_ref in enumerate(lead_refs):
         where = pl.ds(pl.multiple_of(lax.rem(core + s, owners) * width, width), width)
-        for g in range(panel_ref.shape[0] // TILE):
+        for g in range(lead.shape[0] // TILE):
             lead[g * TILE : (g + 1) * TILE, where] = decode(lead_ref, g * (TILE + SUB), TILE)
-    inverse = split(inverse_ref[...])
-    factor_ref[...] = product(inverse, split(panel_ref[...]), PLAIN)
-    row_ref[...] = product(inverse, split(lead[...]), PLAIN)
+    row_ref[...] = product(split(inverse_ref[...]), split(lead[...]), PLAIN)
 
 
 def update_kernel(owners, width, factor_ref, row_ref, own_ref, *refs):
@@ -551,12 +553,15 @@
         1,
     )
     rest_codes = exchange(rest_codes)
-    factor_rows, row_factor = call(
+    factor_rows = call(
+        factor_rows_kernel, shaped(PANEL, per_block, F32), (inverse, panel), limit=12
+    )
+    row_factor = call(
         rows_kernel,
-        (shaped(PANEL, per_block, F32), shaped(PANEL, PANEL, F32)),
-        (inverse, panel, *beside(lead)),
+        shaped(PANEL, PANEL, F32),
+        (inverse, *beside(lead)),
         [pltpu.VMEM((PANEL, PANEL), F32)],
-        14,
+        10,
     )
     return call(
         functools.partial(update_kernel, owners, row_dev),

time: 169 us -> 160 us (0.947)
  the two profiles are of different devices: /device:TPU:22 before, /device:TPU:21 now
where the time goes in v2:
time: 160 us
  starting transfers between devices  68.5 us (43%)
  Pallas kernels  52.2 us (33%)
  waiting for transfers between devices  38 us (24%)
    pallas_call x17, Pallas kernels, call(): pl.pallas_call(kernel, out_shape=out_shape, in_specs=[in_smem()] * scalar...  32.7 us
    ppermute x21, starting transfers between devices, exchange(): lax.ppermute(code, 'cone', [(i, i ^ u) for i in range(cones)])  25.7 us
    ppermute x8, starting transfers between devices, along(): return lax.ppermute(value, 'con', pairs)  22.6 us
    ppermute x8, waiting for transfers between devices, along(): return lax.ppermute(value, 'con', pairs)  22.6 us
    pallas_call x2, Pallas kernels, eliminate(): pl.pallas_call(functools.partial(eliminate_kernel, first, last), out_shap...  18.3 us
    ppermute x6, starting transfers between devices, beside(): swaps.append(lax.ppermute(value, 'con', pairs))  15.7 us
    ppermute x21, waiting for transfers between devices, exchange(): lax.ppermute(code, 'cone', [(i, i ^ u) for i in range(cones)])  15.4 us
    ppermute x3, starting transfers between devices, shards(): leads.append(lax.ppermute(lead, ('cone', 'con'), pairs))  4.57 us
  transfers between devices with their start and end apart: 38, of which 9 were waited for; matrix products, arithmetic and copies ran while one was open for 0% of the time, Pallas kernels for 30%

profile of v2, /device:TPU:21, one launch (start us, length us, event | category | flops | bytes accessed | tf_op | source)
XLA Modules:
  0.0 159.8 jit_solution(14017240886492534387)
XLA Ops:
  0.0 0.7 copy-done.3
  0.7 1.3 mask_rows.1.refs_0_
  1.9 1.4 collective-permute-start.11
  3.3 1.0 collective-permute-start
  4.2 1.9 %collective-permute-start.17 = (bf16[256,1024]{1,0:T(8,128)(2,1)S(1)}, bf16[256,1024]{1,0:T(8,128)(2,1)S(1)}, u32[]{:S(2)}, u32[]{:S(2)}) collective-permute-start(bf16[256,1024]{1,0:T(8,128)(2,1)S(1)} %mask_rows.1.refs_0_), channel_id=1, source_target_pairs={{2,4},{3,5},{4,2},{5,3},{10,12},{11,13},{12,10},{13,11},{18,20},{1... | collective-permute-start | bytes 1572872 | tf_op jit(solution)/shard_map/ppermute | solution.py:430
  6.2 0.7 collective-permute-start.16
  6.9 7.9 %collective-permute-done.11.refs_0_ = bf16[256,1024]{1,0:T(8,128)(2,1)S(1)} collective-permute-done((bf16[256,1024]{1,0:T(8,128)(2,1)S(1)}, bf16[256,1024]{1,0:T(8,128)(2,1)S(1)}, u32[]{:S(2)}, u32[]{:S(2)}) %collective-permute-start.11) | collective-permute-done | bytes 524320 | tf_op jit(solution)/shard_map/ppermute | solution.py:430
  14.8 2.1 %collective-permute-start.18 = (bf16[256,1024]{1,0:T(8,128)(2,1)S(1)}, bf16[256,1024]{1,0:T(8,128)(2,1)S(1)}, u32[]{:S(2)}, u32[]{:S(2)}) collective-permute-start(bf16[256,1024]{1,0:T(8,128)(2,1)S(1)} %collective-permute-done.11.refs_0_), channel_id=1, source_target_pairs={{2,4},{3,5},{4,2},{5,3},{10,12},{11,13},{12,10},{13,11},{18,20},{1... | collective-permute-start | bytes 1572872 | tf_op jit(solution)/shard_map/ppermute | solution.py:430
  16.9 5.7 %shard_map.55 = (f32[128,1024]{1,0:T(8,128)S(1)}, s16[136,1024]{1,0:T(8,128)(2,1)S(1)}, s16[136,1024]{1,0:T(8,128)(2,1)S(1)}, s16[136,1024]{1,0:T(8,128)(2,1)S(1...) custom-call(s32[1,8]{1,0:T(1,128)S(1)} %copy-done.4, bf16[256,1024]{1,0:T(8,128)(2,1)S(1)} %mask_rows.1.refs_0_, ...), custom_call_target="tpu_custom_call" | custom-call | tf_op jit(solution)/shard_map/pallas_call | solution.py:366
  22.6 1.3 collective-permute-start.8
  23.9 3.3 %collective-permute-start.12 = (bf16[256,1024]{1,0:T(8,128)(2,1)S(1)}, bf16[256,1024]{1,0:T(8,128)(2,1)S(1)}, u32[]{:S(2)}, u32[]{:S(2)}) collective-permute-start(bf16[256,1024]{1,0:T(8,128)(2,1)S(1)} %shard_map.61.refs_0_), channel_id=1, source_target_pairs={{0,1},{1,0},{2,3},{3,2},{4,5},{5,4},{6,7},{7,6},{8,9},{9,8},{10,11... | collective-permute-start | bytes 1572872 | tf_op jit(solution)/shard_map/ppermute | solution.py:440
  27.2 3.6 %collective-permute-done.17.refs_1_.refs_0_ = bf16[256,1024]{1,0:T(8,128)(2,1)S(1)} collective-permute-done((bf16[256,1024]{1,0:T(8,128)(2,1)S(1)}, bf16[256,1024]{1,0:T(8,128)(2,1)S(1)}, u32[]{:S(2)}, u32[]{:S(2)}) %collective-permute-start.17) | collective-permute-done | bytes 524320 | tf_op jit(solution)/shard_map/ppermute | solution.py:430
  30.8 0.2 collective-permute-start.9
  31.1 11.0 %collective-permute-done.18.refs_2_ = bf16[256,1024]{1,0:T(8,128)(2,1)S(1)} collective-permute-done((bf16[256,1024]{1,0:T(8,128)(2,1)S(1)}, bf16[256,1024]{1,0:T(8,128)(2,1)S(1)}, u32[]{:S(2)}, u32[]{:S(2)}) %collective-permute-start.18) | collective-permute-done | bytes 524320 | tf_op jit(solution)/shard_map/ppermute | solution.py:430
  42.1 0.9 collective-permute-start.19
  43.0 1.2 collective-permute-start.10
  44.2 1.2 collective-permute-start.3
  45.4 13.7 %collective-permute-start.30 = (bf16[256,1024]{1,0:T(8,128)(2,1)S(1)}, bf16[256,1024]{1,0:T(8,128)(2,1)S(1)}, u32[]{:S(2)}, u32[]{:S(2)}) collective-permute-start(bf16[256,1024]{1,0:T(8,128)(2,1)S(1)} %collective-permute-done.17.refs_1_.refs_0_), channel_id=1, source_target_pairs={{2,0},{3,1},{4,6},{5,7},{10,8},{11,9},{12,14},{13,15},{18,16},{19,... | collective-permute-start | bytes 1572872 | tf_op jit(solution)/shard_map/ppermute | solution.py:430
  59.1 0.3 collective-permute-start.2
  59.4 0.2 collective-permute-start.1
  59.7 5.5 %shard_map.62 = (f32[128,1024]{1,0:T(8,128)S(1)}, s16[136,1024]{1,0:T(8,128)(2,1)S(1)}, s16[136,1024]{1,0:T(8,128)(2,1)S(1)}, s16[136,1024]{1,0:T(8,128)(2,1)S(1)}) custom-call(s32[1,8]{1,0:T(1,128)S(1)} %copy-done.4, bf16[256,1024]{1,0:T(8,128)(2,1)S(1)} %shard_map.61.refs_0_, bf16[256,1024]{1,0:T(8,128)(2,1)S(1)} %collective-permute-done.12.refs_1_, ...), custom_call_target="tpu_custom_call" | custom-call | tf_op jit(solution)/shard_map/pallas_call | solution.py:366
  65.3 1.3 collective-permute-start.13
  66.5 1.2 collective-permute-start.14
  67.8 5.6 %shard_map.64 = (f32[128,1024]{1,0:T(8,128)S(1)}, s16[136,1024]{1,0:T(8,128)(2,1)S(1)}, s16[136,1024]{1,0:T(8,128)(2,1)S(1)}, s16[136,1024]{1,0:T(8,128)(2,1)S(1)}) custom-call(s32[1,8]{1,0:T(1,128)S(1)} %copy-done.4, bf16[256,1024]{1,0:T(8,128)(2,1)S(1)} %shard_map.63.refs_0_, bf16[256,1024]{1,0:T(8,128)(2,1)S(1)} %collective-permute-done.19.refs_1_, ...), custom_call_target="tpu_custom_call" | custom-call | tf_op jit(solution)/shard_map/pallas_call | solution.py:366
  73.4 0.2 collective-permute-start.15
  73.6 1.2 collective-permute-start.20
  74.8 1.2 collective-permute-start.21
  76.1 0.2 collective-permute-start.22
  76.3 3.5 %collective-permute-start.31 = (bf16[256,1024]{1,0:T(8,128)(2,1)S(1)}, bf16[256,1024]{1,0:T(8,128)(2,1)S(1)}, u32[]{:S(2)}, u32[]{:S(2)}) collective-permute-start(bf16[256,1024]{1,0:T(8,128)(2,1)S(1)} %shard_map.70.refs_0_), channel_id=1, source_target_pairs={{0,1},{1,0},{2,3},{3,2},{4,5},{5,4},{6,7},{7,6},{8,9},{9,8},{10,11... | collective-permute-start | bytes 1572872 | tf_op jit(solution)/shard_map/ppermute | solution.py:440
  79.9 0.4 shard_map.56.refs_0_
  80.2 0.1 collective-permute-done.15.refs_7_
  80.3 0.7 collective-permute-start.6
  81.0 4.3 %collective-permute-done.20.refs_9_ = s16[136,1024]{1,0:T(8,128)(2,1)S(1)} collective-permute-done((s16[136,1024]{1,0:T(8,128)(2,1)S(1)}, s16[136,1024]{1,0:T(8,128)(2,1)S(1)}, u32[]{:S(2)}, u32[]{:S(2)}) %collective-permute-start.20) | collective-permute-done | bytes 278560 | tf_op jit(solution)/shard_map/ppermute | solution.py:424
  85.2 5.7 %collective-permute-done.21.refs_10_ = s16[136,1024]{1,0:T(8,128)(2,1)S(1)} collective-permute-done((s16[136,1024]{1,0:T(8,128)(2,1)S(1)}, s16[136,1024]{1,0:T(8,128)(2,1)S(1)}, u32[]{:S(2)}, u32[]{:S(2)}) %collective-permute-start.21) | collective-permute-done | bytes 278560 | tf_op jit(solution)/shard_map/ppermute | solution.py:424
  91.0 1.3 collective-permute-done.22.refs_11_
  92.2 0.4 shard_map.65
  92.6 0.2 collective-permute-start.25
  92.8 1.3 collective-permute-start.24
  94.1 1.2 collective-permute-start.23
  95.3 1.5 collective-permute-start.5
  96.8 5.5 %shard_map.71 = (f32[128,1024]{1,0:T(8,128)S(1)}, s16[136,1024]{1,0:T(8,128)(2,1)S(1)}, s16[136,1024]{1,0:T(8,128)(2,1)S(1)}, s16[136,1024]{1,0:T(8,128)(2,1)S(1)}) custom-call(s32[1,8]{1,0:T(1,128)S(1)} %copy-done.4, bf16[256,1024]{1,0:T(8,128)(2,1)S(1)} %shard_map.70.refs_0_, bf16[256,1024]{1,0:T(8,128)(2,1)S(1)} %collective-permute-done.31.refs_1_, ...), custom_call_target="tpu_custom_call" | custom-call | tf_op jit(solution)/shard_map/pallas_call | solution.py:366
  102.4 0.0 copy-start.5
  102.4 0.7 collective-permute-start.4
  103.1 0.3 collective-permute-start.32
  103.4 3.0 %collective-permute-done.24.refs_1_ = s16[136,1024]{1,0:T(8,128)(2,1)S(1)} collective-permute-done((s16[136,1024]{1,0:T(8,128)(2,1)S(1)}, s16[136,1024]{1,0:T(8,128)(2,1)S(1)}, u32[]{:S(2)}, u32[]{:S(2)}) %collective-permute-start.24) | collective-permute-done | bytes 278560 | tf_op jit(solution)/shard_map/ppermute | solution.py:424
  106.4 0.9 collective-permute-start.33
  107.4 1.4 collective-permute-start.34
  108.8 0.4 shard_map.66
  109.2 1.3 collective-permute-start.28
  110.5 2.0 %collective-permute-start.27 = (s16[544,256]{1,0:T(8,128)(2,1)S(1)}, s16[544,256]{1,0:T(8,128)(2,1)S(1)}, u32[]{:S(2)}, u32[]{:S(2)}) collective-permute-start(s16[544,256]{1,0:T(8,128)(2,1)S(1)} %get-tuple-element.58.refs_0_), channel_id=1, source_target_pairs={{10,14},{11,15},{20,16},{21,17},{30,26},{31,27}} | collective-permute-start | bytes 835592 | tf_op jit(solution)/shard_map/ppermute | solution.py:540
  112.5 1.3 collective-permute-start.26
  113.9 1.0 collective-permute-done.33.refs_14_
  114.9 6.6 %collective-permute-start.7 = (s16[544,256]{1,0:T(8,128)(2,1)S(1)}, s16[544,256]{1,0:T(8,128)(2,1)S(1)}, u32[]{:S(2)}, u32[]{:S(2)}) collective-permute-start(s16[544,256]{1,0:T(8,128)(2,1)S(1)} %shard_map.57.refs_0_), channel_id=1, source_target_pairs={{0,1},{1,0},{2,3},{3,2},{4,5},{5,4},{6,7},{7,6},{8,9},{9,8},{10,11... | collective-permute-start | bytes 835592 | tf_op jit(solution)/shard_map/ppermute | solution.py:440
  121.5 1.6 shard_map.72
  123.1 1.2 collective-permute-start.35
  124.3 0.3 shard_map.68.refs_0_
  124.6 0.4 collective-permute-start.29
  125.0 9.3 %collective-permute-start.37 = (s16[136,1024]{1,0:T(8,128)(2,1)S(1)}, s16[136,1024]{1,0:T(8,128)(2,1)S(1)}, u32[]{:S(2)}, u32[]{:S(2)}) collective-permute-start(s16[136,1024]{1,0:T(8,128)(2,1)S(1)} %get-tuple-element.66), channel_id=1, source_target_pairs={{0,24},{8,16},{16,8},{24,0},{1,25},{9,17},{17,9},{25,1},{2,26},{10... | collective-permute-start | bytes 835592 | tf_op jit(solution)/shard_map/ppermute | solution.py:424
  134.3 0.7 shard_map.58
  135.0 9.9 %shard_map.59 = (f32[512,512]{1,0:T(8,128)S(1)}, f32[512,512]{1,0:T(8,128)S(1)}) custom-call(f32[512,512]{1,0:T(8,128)S(1)} %get-tuple-element.38.work_in, f32[512,512]{1,0:T(8,128)S(1)} %get-tuple-element.39.x_in), custom_call_target="tpu_custom_call", output_to_operand_aliasing={{0}: (0, {}), {1}: (1, {})} | custom-call | tf_op jit(solution)/shard_map/pallas_call | solution.py:128
  144.9 8.4 %shard_map.60 = (f32[512,512]{1,0:T(8,128)S(1)}, f32[512,512]{1,0:T(8,128)S(1)}) custom-call(f32[512,512]{1,0:T(8,128)S(1)} %get-tuple-element.40.work_in, f32[512,512]{1,0:T(8,128)S(1)} %get-tuple-element.41.x_in), custom_call_target="tpu_custom_call", output_to_operand_aliasing={{0}: (0, {}), {1}: (1, {})} | custom-call | tf_op jit(solution)/shard_map/pallas_call | solution.py:128
  153.3 1.9 %shard_map.67.factor_ref = f32[512,1024]{1,0:T(8,128)S(1)} custom-call(f32[512,512]{1,0:T(8,128)S(1)} %get-tuple-element.42.inverse_ref, f32[512,1024]{1,0:T(8,128)S(1)} %get-tuple-element.57.panel_ref), custom_call_target="tpu_custom_call" | custom-call | tf_op jit(solution)/shard_map/pallas_call | solution.py:366
  155.2 1.2 shard_map.69.row_ref
  156.5 3.4 %shard_map.73 = f32[512,1024]{1,0:T(8,128)} custom-call(f32[512,1024]{1,0:T(8,128)S(1)} %shard_map.67.factor_ref, f32[512,512]{1,0:T(8,128)S(1)} %shard_map.69.row_ref, f32[128,1024]{1,0:T(8,128)S(1)} %get-tuple-element.63.own_ref, s16[136,1024]{1,0:T(8,128)(2,1)S(1)} %collective-permute-done.35.refs_0_, ...), custom_call_target="tpu_custom_call" | custom-call | tf_op jit(solution)/shard_map/pallas_call | solution.py:366
  (44 shorter events, 0.3 us)
Async XLA Ops:
  0.0 0.7 copy-start.3
  0.7 16.2 %copy-start = (bf16[1,1024,1024]{2,1,0:T(8,128)(2,1)S(1)}, bf16[1,1024,1024]{2,1,0:T(8,128)(2,1)}, u32[]{:S(2)}) copy-start(bf16[1,1024,1024]{2,1,0:T(8,128)(2,1)} %param.5) | copy-start | bytes 6291460
  0.7 16.2 %copy-start.1 = (bf16[1,1024,1024]{2,1,0:T(8,128)(2,1)S(1)}, bf16[1,1024,1024]{2,1,0:T(8,128)(2,1)}, u32[]{:S(2)}) copy-start(bf16[1,1024,1024]{2,1,0:T(8,128)(2,1)} %param.6) | copy-start | bytes 6291460
  0.7 16.2 %copy-start.2 = (bf16[1,1024,1024]{2,1,0:T(8,128)(2,1)S(1)}, bf16[1,1024,1024]{2,1,0:T(8,128)(2,1)}, u32[]{:S(2)}) copy-start(bf16[1,1024,1024]{2,1,0:T(8,128)(2,1)} %param.7) | copy-start | bytes 6291460
  0.7 16.3 %copy-start.4 = (s32[1,8]{1,0:T(1,128)S(1)}, s32[1,8]{1,0:T(1,128)}, u32[]{:S(2)}) copy-start(s32[1,8]{1,0:T(1,128)} %touches_ref.9) | copy-start | bytes 100
  1.9 12.9 %collective-permute-start.11 = (bf16[256,1024]{1,0:T(8,128)(2,1)S(1)}, bf16[256,1024]{1,0:T(8,128)(2,1)S(1)}, u32[]{:S(2)}, u32[]{:S(2)}) collective-permute-start(bf16[256,1024]{1,0:T(8,128)(2,1)S(1)} %mask_rows.1.refs_0_), channel_id=1, source_target_pairs={{0,2},{1,3},{2,0},{3,1},{4,6},{5,7},{6,4},{7,5},{8,10},{9,11},{10,... | collective-permute-start | bytes 1572872 | tf_op jit(solution)/shard_map/ppermute | solution.py:430
  3.3 13.6 %collective-permute-start = (bf16[256,1024]{1,0:T(8,128)(2,1)S(1)}, bf16[256,1024]{1,0:T(8,128)(2,1)S(1)}, u32[]{:S(2)}, u32[]{:S(2)}) collective-permute-start(bf16[256,1024]{1,0:T(8,128)(2,1)S(1)} %mask_rows.1.refs_0_), channel_id=1, source_target_pairs={{0,1},{1,0},{2,3},{3,2},{4,5},{5,4},{6,7},{7,6},{8,9},{9,8},{10,11... | collective-permute-start | bytes 1572872 | tf_op jit(solution)/shard_map/ppermute | solution.py:440
  4.2 26.6 %collective-permute-start.17 = (bf16[256,1024]{1,0:T(8,128)(2,1)S(1)}, bf16[256,1024]{1,0:T(8,128)(2,1)S(1)}, u32[]{:S(2)}, u32[]{:S(2)}) collective-permute-start(bf16[256,1024]{1,0:T(8,128)(2,1)S(1)} %mask_rows.1.refs_0_), channel_id=1, source_target_pairs={{2,4},{3,5},{4,2},{5,3},{10,12},{11,13},{12,10},{13,11},{18,20},{1... | collective-permute-start | bytes 1572872 | tf_op jit(solution)/shard_map/ppermute | solution.py:430
  6.2 24.9 %collective-permute-start.16 = (bf16[256,1024]{1,0:T(8,128)(2,1)S(1)}, bf16[256,1024]{1,0:T(8,128)(2,1)S(1)}, u32[]{:S(2)}, u32[]{:S(2)}) collective-permute-start(bf16[256,1024]{1,0:T(8,128)(2,1)S(1)} %mask_rows.1.refs_0_), channel_id=1, source_target_pairs={{0,6},{1,7},{6,0},{7,1},{8,14},{9,15},{14,8},{15,9},{16,22},{17,23... | collective-permute-start | bytes 1572872 | tf_op jit(solution)/shard_map/ppermute | solution.py:430
  14.8 27.3 %collective-permute-start.18 = (bf16[256,1024]{1,0:T(8,128)(2,1)S(1)}, bf16[256,1024]{1,0:T(8,128)(2,1)S(1)}, u32[]{:S(2)}, u32[]{:S(2)}) collective-permute-start(bf16[256,1024]{1,0:T(8,128)(2,1)S(1)} %collective-permute-done.11.refs_0_), channel_id=1, source_target_pairs={{2,4},{3,5},{4,2},{5,3},{10,12},{11,13},{12,10},{13,11},{18,20},{1... | collective-permute-start | bytes 1572872 | tf_op jit(solution)/shard_map/ppermute | solution.py:430
  22.6 21.6 %collective-permute-start.8 = (s16[136,1024]{1,0:T(8,128)(2,1)S(1)}, s16[136,1024]{1,0:T(8,128)(2,1)S(1)}, u32[]{:S(2)}, u32[]{:S(2)}) collective-permute-start(s16[136,1024]{1,0:T(8,128)(2,1)S(1)} %get-tuple-element.44), channel_id=1, source_target_pairs={{0,8},{8,0},{16,24},{24,16},{1,9},{9,1},{17,25},{25,17},{2,10},{10... | collective-permute-start | bytes 835592 | tf_op jit(solution)/shard_map/ppermute | solution.py:424
  23.9 35.5 %collective-permute-start.12 = (bf16[256,1024]{1,0:T(8,128)(2,1)S(1)}, bf16[256,1024]{1,0:T(8,128)(2,1)S(1)}, u32[]{:S(2)}, u32[]{:S(2)}) collective-permute-start(bf16[256,1024]{1,0:T(8,128)(2,1)S(1)} %shard_map.61.refs_0_), channel_id=1, source_target_pairs={{0,1},{1,0},{2,3},{3,2},{4,5},{5,4},{6,7},{7,6},{8,9},{9,8},{10,11... | collective-permute-start | bytes 1572872 | tf_op jit(solution)/shard_map/ppermute | solution.py:440
  30.8 14.6 %collective-permute-start.9 = (s16[136,1024]{1,0:T(8,128)(2,1)S(1)}, s16[136,1024]{1,0:T(8,128)(2,1)S(1)}, u32[]{:S(2)}, u32[]{:S(2)}) collective-permute-start(s16[136,1024]{1,0:T(8,128)(2,1)S(1)} %get-tuple-element.45), channel_id=1, source_target_pairs={{0,16},{8,24},{16,0},{24,8},{1,17},{9,25},{17,1},{25,9},{2,18},{10... | collective-permute-start | bytes 835592 | tf_op jit(solution)/shard_map/ppermute | solution.py:424
  42.1 24.4 %collective-permute-start.19 = (bf16[256,1024]{1,0:T(8,128)(2,1)S(1)}, bf16[256,1024]{1,0:T(8,128)(2,1)S(1)}, u32[]{:S(2)}, u32[]{:S(2)}) collective-permute-start(bf16[256,1024]{1,0:T(8,128)(2,1)S(1)} %shard_map.63.refs_0_), channel_id=1, source_target_pairs={{0,1},{1,0},{2,3},{3,2},{4,5},{5,4},{6,7},{7,6},{8,9},{9,8},{10,11... | collective-permute-start | bytes 1572872 | tf_op jit(solution)/shard_map/ppermute | solution.py:440
  43.0 16.1 %collective-permute-start.10 = (s16[136,1024]{1,0:T(8,128)(2,1)S(1)}, s16[136,1024]{1,0:T(8,128)(2,1)S(1)}, u32[]{:S(2)}, u32[]{:S(2)}) collective-permute-start(s16[136,1024]{1,0:T(8,128)(2,1)S(1)} %get-tuple-element.46), channel_id=1, source_target_pairs={{0,24},{8,16},{16,8},{24,0},{1,25},{9,17},{17,9},{25,1},{2,26},{10... | collective-permute-start | bytes 835592 | tf_op jit(solution)/shard_map/ppermute | solution.py:424
  44.2 21.0 %collective-permute-start.3 = (s16[544,256]{1,0:T(8,128)(2,1)S(1)}, s16[544,256]{1,0:T(8,128)(2,1)S(1)}, u32[]{:S(2)}, u32[]{:S(2)}) collective-permute-start(s16[544,256]{1,0:T(8,128)(2,1)S(1)} %get-tuple-element.37), channel_id=1, source_target_pairs={{0,24},{8,16},{16,8},{24,0},{1,25},{9,17},{17,9},{25,1},{2,26},{10... | collective-permute-start | bytes 835592 | tf_op jit(solution)/shard_map/ppermute | solution.py:424
  45.4 29.4 %collective-permute-start.30 = (bf16[256,1024]{1,0:T(8,128)(2,1)S(1)}, bf16[256,1024]{1,0:T(8,128)(2,1)S(1)}, u32[]{:S(2)}, u32[]{:S(2)}) collective-permute-start(bf16[256,1024]{1,0:T(8,128)(2,1)S(1)} %collective-permute-done.17.refs_1_.refs_0_), channel_id=1, source_target_pairs={{2,0},{3,1},{4,6},{5,7},{10,8},{11,9},{12,14},{13,15},{18,16},{19,... | collective-permute-start | bytes 1572872 | tf_op jit(solution)/shard_map/ppermute | solution.py:430
  59.1 14.2 %collective-permute-start.2 = (s16[544,256]{1,0:T(8,128)(2,1)S(1)}, s16[544,256]{1,0:T(8,128)(2,1)S(1)}, u32[]{:S(2)}, u32[]{:S(2)}) collective-permute-start(s16[544,256]{1,0:T(8,128)(2,1)S(1)} %get-tuple-element.37), channel_id=1, source_target_pairs={{0,16},{8,24},{16,0},{24,8},{1,17},{9,25},{17,1},{25,9},{2,18},{10... | collective-permute-start | bytes 835592 | tf_op jit(solution)/shard_map/ppermute | solution.py:424
  59.4 14.2 %collective-permute-start.1 = (s16[544,256]{1,0:T(8,128)(2,1)S(1)}, s16[544,256]{1,0:T(8,128)(2,1)S(1)}, u32[]{:S(2)}, u32[]{:S(2)}) collective-permute-start(s16[544,256]{1,0:T(8,128)(2,1)S(1)} %get-tuple-element.37), channel_id=1, source_target_pairs={{0,8},{8,0},{16,24},{24,16},{1,9},{9,1},{17,25},{25,17},{2,10},{10... | collective-permute-start | bytes 835592 | tf_op jit(solution)/shard_map/ppermute | solution.py:424
  65.3 10.8 %collective-permute-start.13 = (s16[136,1024]{1,0:T(8,128)(2,1)S(1)}, s16[136,1024]{1,0:T(8,128)(2,1)S(1)}, u32[]{:S(2)}, u32[]{:S(2)}) collective-permute-start(s16[136,1024]{1,0:T(8,128)(2,1)S(1)} %get-tuple-element.48), channel_id=1, source_target_pairs={{0,8},{8,0},{16,24},{24,16},{1,9},{9,1},{17,25},{25,17},{2,10},{10... | collective-permute-start | bytes 835592 | tf_op jit(solution)/shard_map/ppermute | solution.py:424
  66.5 9.8 %collective-permute-start.14 = (s16[136,1024]{1,0:T(8,128)(2,1)S(1)}, s16[136,1024]{1,0:T(8,128)(2,1)S(1)}, u32[]{:S(2)}, u32[]{:S(2)}) collective-permute-start(s16[136,1024]{1,0:T(8,128)(2,1)S(1)} %get-tuple-element.49), channel_id=1, source_target_pairs={{0,16},{8,24},{16,0},{24,8},{1,17},{9,25},{17,1},{25,9},{2,18},{10... | collective-permute-start | bytes 835592 | tf_op jit(solution)/shard_map/ppermute | solution.py:424
  73.4 6.9 %collective-permute-start.15 = (s16[136,1024]{1,0:T(8,128)(2,1)S(1)}, s16[136,1024]{1,0:T(8,128)(2,1)S(1)}, u32[]{:S(2)}, u32[]{:S(2)}) collective-permute-start(s16[136,1024]{1,0:T(8,128)(2,1)S(1)} %get-tuple-element.50), channel_id=1, source_target_pairs={{0,24},{8,16},{16,8},{24,0},{1,25},{9,17},{17,9},{25,1},{2,26},{10... | collective-permute-start | bytes 835592 | tf_op jit(solution)/shard_map/ppermute | solution.py:424
  73.6 11.6 %collective-permute-start.20 = (s16[136,1024]{1,0:T(8,128)(2,1)S(1)}, s16[136,1024]{1,0:T(8,128)(2,1)S(1)}, u32[]{:S(2)}, u32[]{:S(2)}) collective-permute-start(s16[136,1024]{1,0:T(8,128)(2,1)S(1)} %get-tuple-element.52), channel_id=1, source_target_pairs={{0,8},{8,0},{16,24},{24,16},{1,9},{9,1},{17,25},{25,17},{2,10},{10... | collective-permute-start | bytes 835592 | tf_op jit(solution)/shard_map/ppermute | solution.py:424
  74.8 16.1 %collective-permute-start.21 = (s16[136,1024]{1,0:T(8,128)(2,1)S(1)}, s16[136,1024]{1,0:T(8,128)(2,1)S(1)}, u32[]{:S(2)}, u32[]{:S(2)}) collective-permute-start(s16[136,1024]{1,0:T(8,128)(2,1)S(1)} %get-tuple-element.53), channel_id=1, source_target_pairs={{0,16},{8,24},{16,0},{24,8},{1,17},{9,25},{17,1},{25,9},{2,18},{10... | collective-permute-start | bytes 835592 | tf_op jit(solution)/shard_map/ppermute | solution.py:424
  76.1 16.1 %collective-permute-start.22 = (s16[136,1024]{1,0:T(8,128)(2,1)S(1)}, s16[136,1024]{1,0:T(8,128)(2,1)S(1)}, u32[]{:S(2)}, u32[]{:S(2)}) collective-permute-start(s16[136,1024]{1,0:T(8,128)(2,1)S(1)} %get-tuple-element.54), channel_id=1, source_target_pairs={{0,24},{8,16},{16,8},{24,0},{1,25},{9,17},{17,9},{25,1},{2,26},{10... | collective-permute-start | bytes 835592 | tf_op jit(solution)/shard_map/ppermute | solution.py:424
  76.3 19.0 %collective-permute-start.31 = (bf16[256,1024]{1,0:T(8,128)(2,1)S(1)}, bf16[256,1024]{1,0:T(8,128)(2,1)S(1)}, u32[]{:S(2)}, u32[]{:S(2)}) collective-permute-start(bf16[256,1024]{1,0:T(8,128)(2,1)S(1)} %shard_map.70.refs_0_), channel_id=1, source_target_pairs={{0,1},{1,0},{2,3},{3,2},{4,5},{5,4},{6,7},{7,6},{8,9},{9,8},{10,11... | collective-permute-start | bytes 1572872 | tf_op jit(solution)/shard_map/ppermute | solution.py:440
  80.3 22.1 %collective-permute-start.6 = (s16[544,256]{1,0:T(8,128)(2,1)S(1)}, s16[544,256]{1,0:T(8,128)(2,1)S(1)}, u32[]{:S(2)}, u32[]{:S(2)}) collective-permute-start(s16[544,256]{1,0:T(8,128)(2,1)S(1)} %shard_map.56.refs_0_), channel_id=1, source_target_pairs={{0,6},{1,7},{8,14},{9,15},{16,22},{17,23},{24,30},{25,31}} | collective-permute-start | bytes 835592 | tf_op jit(solution)/shard_map/ppermute | solution.py:430
  92.6 10.5 %collective-permute-start.25 = (s16[136,1024]{1,0:T(8,128)(2,1)S(1)}, s16[136,1024]{1,0:T(8,128)(2,1)S(1)}, u32[]{:S(2)}, u32[]{:S(2)}) collective-permute-start(s16[136,1024]{1,0:T(8,128)(2,1)S(1)} %get-tuple-element.56), channel_id=1, source_target_pairs={{0,24},{8,16},{16,8},{24,0},{1,25},{9,17},{17,9},{25,1},{2,26},{10... | collective-permute-start | bytes 835592 | tf_op jit(solution)/shard_map/ppermute | solution.py:424
  92.8 13.7 %collective-permute-start.24 = (s16[136,1024]{1,0:T(8,128)(2,1)S(1)}, s16[136,1024]{1,0:T(8,128)(2,1)S(1)}, u32[]{:S(2)}, u32[]{:S(2)}) collective-permute-start(s16[136,1024]{1,0:T(8,128)(2,1)S(1)} %get-tuple-element.56), channel_id=1, source_target_pairs={{0,16},{8,24},{16,0},{24,8},{1,17},{9,25},{17,1},{25,9},{2,18},{10... | collective-permute-start | bytes 835592 | tf_op jit(solution)/shard_map/ppermute | solution.py:424
  94.1 13.3 %collective-permute-start.23 = (s16[136,1024]{1,0:T(8,128)(2,1)S(1)}, s16[136,1024]{1,0:T(8,128)(2,1)S(1)}, u32[]{:S(2)}, u32[]{:S(2)}) collective-permute-start(s16[136,1024]{1,0:T(8,128)(2,1)S(1)} %get-tuple-element.56), channel_id=1, source_target_pairs={{0,8},{8,0},{16,24},{24,16},{1,9},{9,1},{17,25},{25,17},{2,10},{10... | collective-permute-start | bytes 835592 | tf_op jit(solution)/shard_map/ppermute | solution.py:424
  95.3 13.9 %collective-permute-start.5 = (s16[544,256]{1,0:T(8,128)(2,1)S(1)}, s16[544,256]{1,0:T(8,128)(2,1)S(1)}, u32[]{:S(2)}, u32[]{:S(2)}) collective-permute-start(s16[544,256]{1,0:T(8,128)(2,1)S(1)} %shard_map.56.refs_0_), channel_id=1, source_target_pairs={{0,4},{1,5},{8,12},{9,13},{16,20},{17,21},{24,28},{25,29}} | collective-permute-start | bytes 835592 | tf_op jit(solution)/shard_map/ppermute | solution.py:430
  102.4 19.1 %copy-start.5 = (s32[4,4]{1,0:T(4,128)S(1)}, s32[4,4]{1,0:T(4,128)}, u32[]{:S(2)}) copy-start(s32[4,4]{1,0:T(4,128)} %constant.2.clone.order_ref) | copy-start | bytes 196
  102.4 8.1 %collective-permute-start.4 = (s16[544,256]{1,0:T(8,128)(2,1)S(1)}, s16[544,256]{1,0:T(8,128)(2,1)S(1)}, u32[]{:S(2)}, u32[]{:S(2)}) collective-permute-start(s16[544,256]{1,0:T(8,128)(2,1)S(1)} %shard_map.56.refs_0_), channel_id=1, source_target_pairs={{0,2},{1,3},{8,10},{9,11},{16,18},{17,19},{24,26},{25,27}} | collective-permute-start | bytes 835592 | tf_op jit(solution)/shard_map/ppermute | solution.py:430
  103.1 9.4 %collective-permute-start.32 = (s16[136,1024]{1,0:T(8,128)(2,1)S(1)}, s16[136,1024]{1,0:T(8,128)(2,1)S(1)}, u32[]{:S(2)}, u32[]{:S(2)}) collective-permute-start(s16[136,1024]{1,0:T(8,128)(2,1)S(1)} %get-tuple-element.60), channel_id=1, source_target_pairs={{0,8},{8,0},{16,24},{24,16},{1,9},{9,1},{17,25},{25,17},{2,10},{10... | collective-permute-start | bytes 835592 | tf_op jit(solution)/shard_map/ppermute | solution.py:424
  106.4 8.4 %collective-permute-start.33 = (s16[136,1024]{1,0:T(8,128)(2,1)S(1)}, s16[136,1024]{1,0:T(8,128)(2,1)S(1)}, u32[]{:S(2)}, u32[]{:S(2)}) collective-permute-start(s16[136,1024]{1,0:T(8,128)(2,1)S(1)} %get-tuple-element.61), channel_id=1, source_target_pairs={{0,16},{8,24},{16,0},{24,8},{1,17},{9,25},{17,1},{25,9},{2,18},{10... | collective-permute-start | bytes 835592 | tf_op jit(solution)/shard_map/ppermute | solution.py:424
  107.4 14.1 %collective-permute-start.34 = (s16[136,1024]{1,0:T(8,128)(2,1)S(1)}, s16[136,1024]{1,0:T(8,128)(2,1)S(1)}, u32[]{:S(2)}, u32[]{:S(2)}) collective-permute-start(s16[136,1024]{1,0:T(8,128)(2,1)S(1)} %get-tuple-element.62), channel_id=1, source_target_pairs={{0,24},{8,16},{16,8},{24,0},{1,25},{9,17},{17,9},{25,1},{2,26},{10... | collective-permute-start | bytes 835592 | tf_op jit(solution)/shard_map/ppermute | solution.py:424
  109.2 15.1 %collective-permute-start.28 = (s16[544,256]{1,0:T(8,128)(2,1)S(1)}, s16[544,256]{1,0:T(8,128)(2,1)S(1)}, u32[]{:S(2)}, u32[]{:S(2)}) collective-permute-start(s16[544,256]{1,0:T(8,128)(2,1)S(1)} %get-tuple-element.58.refs_0_), channel_id=1, source_target_pairs={{10,12},{11,13},{20,18},{21,19},{30,24},{31,25}} | collective-permute-start | bytes 835592 | tf_op jit(solution)/shard_map/ppermute | solution.py:540
  110.5 13.8 %collective-permute-start.27 = (s16[544,256]{1,0:T(8,128)(2,1)S(1)}, s16[544,256]{1,0:T(8,128)(2,1)S(1)}, u32[]{:S(2)}, u32[]{:S(2)}) collective-permute-start(s16[544,256]{1,0:T(8,128)(2,1)S(1)} %get-tuple-element.58.refs_0_), channel_id=1, source_target_pairs={{10,14},{11,15},{20,16},{21,17},{30,26},{31,27}} | collective-permute-start | bytes 835592 | tf_op jit(solution)/shard_map/ppermute | solution.py:540
  112.5 11.8 %collective-permute-start.26 = (s16[544,256]{1,0:T(8,128)(2,1)S(1)}, s16[544,256]{1,0:T(8,128)(2,1)S(1)}, u32[]{:S(2)}, u32[]{:S(2)}) collective-permute-start(s16[544,256]{1,0:T(8,128)(2,1)S(1)} %get-tuple-element.58.refs_0_), channel_id=1, source_target_pairs={{10,8},{11,9},{20,22},{21,23},{30,28},{31,29}} | collective-permute-start | bytes 835592 | tf_op jit(solution)/shard_map/ppermute | solution.py:540
  114.9 19.4 %collective-permute-start.7 = (s16[544,256]{1,0:T(8,128)(2,1)S(1)}, s16[544,256]{1,0:T(8,128)(2,1)S(1)}, u32[]{:S(2)}, u32[]{:S(2)}) collective-permute-start(s16[544,256]{1,0:T(8,128)(2,1)S(1)} %shard_map.57.refs_0_), channel_id=1, source_target_pairs={{0,1},{1,0},{2,3},{3,2},{4,5},{5,4},{6,7},{7,6},{8,9},{9,8},{10,11... | collective-permute-start | bytes 835592 | tf_op jit(solution)/shard_map/ppermute | solution.py:440
  123.1 33.4 %collective-permute-start.35 = (s16[136,1024]{1,0:T(8,128)(2,1)S(1)}, s16[136,1024]{1,0:T(8,128)(2,1)S(1)}, u32[]{:S(2)}, u32[]{:S(2)}) collective-permute-start(s16[136,1024]{1,0:T(8,128)(2,1)S(1)} %get-tuple-element.64), channel_id=1, source_target_pairs={{0,8},{8,0},{16,24},{24,16},{1,9},{9,1},{17,25},{25,17},{2,10},{10... | collective-permute-start | bytes 835592 | tf_op jit(solution)/shard_map/ppermute | solution.py:424
  124.6 30.6 %collective-permute-start.29 = (s16[544,256]{1,0:T(8,128)(2,1)S(1)}, s16[544,256]{1,0:T(8,128)(2,1)S(1)}, u32[]{:S(2)}, u32[]{:S(2)}) collective-permute-start(s16[544,256]{1,0:T(8,128)(2,1)S(1)} %shard_map.68.refs_0_), channel_id=1, source_target_pairs={{0,1},{1,0},{2,3},{3,2},{4,5},{5,4},{6,7},{7,6},{8,9},{9,8},{10,11... | collective-permute-start | bytes 835592 | tf_op jit(solution)/shard_map/ppermute | solution.py:440
  125.0 31.5 %collective-permute-start.36 = (s16[136,1024]{1,0:T(8,128)(2,1)S(1)}, s16[136,1024]{1,0:T(8,128)(2,1)S(1)}, u32[]{:S(2)}, u32[]{:S(2)}) collective-permute-start(s16[136,1024]{1,0:T(8,128)(2,1)S(1)} %get-tuple-element.65), channel_id=1, source_target_pairs={{0,16},{8,24},{16,0},{24,8},{1,17},{9,25},{17,1},{25,9},{2,18},{10... | collective-permute-start | bytes 835592 | tf_op jit(solution)/shard_map/ppermute | solution.py:424
  125.0 31.5 %collective-permute-start.37 = (s16[136,1024]{1,0:T(8,128)(2,1)S(1)}, s16[136,1024]{1,0:T(8,128)(2,1)S(1)}, u32[]{:S(2)}, u32[]{:S(2)}) collective-permute-start(s16[136,1024]{1,0:T(8,128)(2,1)S(1)} %get-tuple-element.66), channel_id=1, source_target_pairs={{0,24},{8,16},{16,8},{24,0},{1,25},{9,17},{17,9},{25,1},{2,26},{10... | collective-permute-start | bytes 835592 | tf_op jit(solution)/shard_map/ppermute | solution.py:424
